TPU v7x, 256 devices: a whole 4x4x8 slice. The times are simulated.
256 devices in a mesh: orb: 64 (over x, z, core), wall: 4 (over y).
Axes of the slice: x: 4, y: 4, z: 8, core: 2. Of those that a mesh axis runs over, the one named last changes fastest.
Arguments:
- fluid_state: float32 [8, 786432], P(None, ('orb', 'wall')), may hold values from -4 to 4, as said below
- ghost_list: int32 [7, 1536], P(None, ('orb', 'wall')), may hold values from 0 to 23, as said below
- pair_list: int32 [6144, 14], P(('orb', 'wall')), may hold values from 0 to 65, as said below
- wall_state: float32 [4, 196608], P(None, ('orb', 'wall')), may hold values from 0 to 0.6, as said below
- wall_count: int32 [1536], P(('orb', 'wall')), may hold values from 1 to 128, as said below
- wall_pairs: int32 [6144, 4], P(('orb', 'wall')), may hold values from 0 to 7, as said below
Outputs:
- density_rate: float32 [786432], P(('orb', 'wall'))
- acceleration: float32 [3, 786432], P(None, ('orb', 'wall'))
- time_step: float32 [], replicated
Inputs may be any that keep to these rules, and one draw needn't show every extreme that they name: `fluid_state`: rows: position from 0 to 0.6, velocity from -4 to 4, density from 0.97 to 1.03, mass from 0.001 to 0.003. `ghost_list`: the 6 entries of one mask and one domain are distinct. `pair_list`: the 14 entries of one block are distinct, and every candidate index is named by some block of each domain. `wall_state`: rows: x and y from 0 to 0.6, z from 0 to 0.15, mass from 0.001 to 0.003. `wall_count`: the live particles fill the first columns of their wall block. `wall_pairs`: the 4 entries of one block are distinct, and every wall candidate index is named by some block of each domain.
All inputs are finite; a program needn't handle non-finite values.
Results may differ from a plain program's by a relative error of at most 0.0003.
Values sent between devices are 32-bit elements; how exact they have to be, the bound alone decides.
A program may use at most 64 MiB of HBM per device.

v0:
```python
import jax
import jax.numpy as jnp
from jax import lax
from jax.sharding import PartitionSpec as P

EB = 1


smoothing = 0.1
support = 0.3
kernel_norm = 21.0 / (2.0 * 3.141592653589793 * support**3)
grad_coeff = -20.0 / support**2 * kernel_norm
tait_coeff = 25.0 / 7.0
visc_coeff = 0.05
cohesion = 2000.0
adhesion = 2000.0
gravity = 9.81
courant = 0.25


def swapped(shard, axis, bit):
    return lax.ppermute(shard, axis, [(i, i ^ 1 << bit) for i in range(lax.axis_size(axis))])


def padded(block, sides, width):
    for axis, dim in sides:
        count = lax.axis_size(axis)
        forward = [(i, i + 1) for i in range(count - 1)]
        backward = [(target, source) for source, target in forward]
        low = lax.ppermute(
            lax.slice_in_dim(block, block.shape[dim] - width, None, axis=dim), axis, forward
        )
        high = lax.ppermute(lax.slice_in_dim(block, 0, width, axis=dim), axis, backward)
        block = jnp.concatenate([low, block, high], axis=dim)
    return block


def kernel_parts(target_pos, source_pos):
    offset = target_pos[None, :, :, None] - source_pos[:, :, None, :]
    dist_sq = jnp.sum(offset * offset, axis=1)
    radius = jnp.sqrt(dist_sq)
    scaled = radius / support
    falloff = jnp.maximum(1.0 - scaled, 0.0)
    cubed = falloff * falloff * falloff
    return (offset, dist_sq, grad_coeff * cubed, cubed * (4.0 * scaled - 1.0))


def pressure_of(density):
    return tait_coeff * (density**7 - 1.0)


def block_terms(target, sources, walls):
    target_pos = target[0:3]
    target_vel = target[3:6]
    target_rho = target[6]
    target_press = pressure_of(target_rho)
    source_rho = sources[:, 6]
    offset, dist_sq, grad_scale, pull = kernel_parts(target_pos, sources[:, 0:3])
    vel_diff = target_vel[None, :, :, None] - sources[:, 3:6][:, :, None, :]
    approach = jnp.sum(vel_diff * offset, axis=1)
    mass_row = sources[:, 7][:, None, :]
    fluid_rate = jnp.sum(mass_row * approach * grad_scale, axis=(0, 2))
    mean_rho = 0.5 * (target_rho[None, :, None] + source_rho[:, None, :])
    viscous = -visc_coeff * jnp.minimum(approach, 0.0) / ((dist_sq + 0.0001) * mean_rho)
    press_term = (
        (target_press / target_rho**2)[None, :, None]
        + (pressure_of(source_rho) / source_rho**2)[:, None, :]
        + viscous
    )
    weight = mass_row * (press_term * grad_scale + cohesion * pull)
    fluid_force = -jnp.sum(weight[:, None] * offset, axis=(0, 3))
    wall_offset, wall_dist, wall_grad, wall_pull = kernel_parts(target_pos, walls[:, 0:3])
    wall_masses = walls[:, 3][:, None, :]
    wall_approach = jnp.sum(target_vel[None, :, :, None] * wall_offset, axis=1)
    wall_rate = jnp.sum(wall_masses * wall_approach * wall_grad, axis=(0, 2))
    own_press = (2.0 * target_press / target_rho**2)[None, :, None]
    wall_weight = wall_masses * (own_press * wall_grad + adhesion * wall_pull)
    wall_force = -jnp.sum(wall_weight[:, None] * wall_offset, axis=(0, 3))
    downward = jnp.array([0.0, 0.0, -gravity], jnp.float32)[:, None]
    return (fluid_rate + wall_rate, fluid_force + wall_force + downward)


def grouped(array):
    return array.reshape((-1, 2) + array.shape[1:])


def per_device(fluid_state, ghost_list, pair_list, wall_state, wall_count, wall_pairs):
    block_total = fluid_state.shape[1] // 128
    own_blocks = jnp.transpose(fluid_state.reshape(8, block_total, 128), (1, 0, 2))
    outgoing = own_blocks[ghost_list]
    arrived = []
    for pattern in range(1, 8):
        parcel = outgoing[pattern - 1]
        for bit_number in range(3):
            if pattern >> bit_number & 1:
                parcel = swapped(parcel, "orb", bit_number)
        arrived.append(parcel)
    ghosts = jnp.stack(arrived)
    candidates = jnp.concatenate([own_blocks, ghosts.reshape(-1, 8, 128)], axis=0)
    alive = (
        (jnp.arange(128, dtype=jnp.int32)[None, :] < wall_count[:, None])
        .astype(jnp.float32)
        .reshape(-1)
    )
    wall_live = jnp.concatenate([wall_state[0:3], wall_state[3:4] * alive[None, :]], axis=0)
    rim_width = EB * 128
    extended = padded(wall_live, (("wall", 1),), rim_width)
    wall_cands = jnp.transpose(extended.reshape(4, -1, 128), (1, 0, 2))

    def per_block(target, pair_row, wall_row):
        return block_terms(target, candidates[pair_row], wall_cands[wall_row])

    def per_group(inputs):
        return jax.vmap(per_block)(inputs[0], inputs[1], inputs[2])

    rates, forces = lax.map(
        per_group, (grouped(own_blocks), grouped(pair_list), grouped(wall_pairs))
    )
    density_rate = rates.reshape(-1)
    acceleration = jnp.transpose(forces.reshape(-1, 3, 128), (1, 0, 2)).reshape(3, -1)
    local_peak = jnp.max(jnp.sqrt(jnp.sum(acceleration * acceleration, axis=0)))
    peak = lax.pmax(local_peak, ("orb", "wall"))
    time_step = courant * jnp.sqrt(smoothing / (peak + 1e-06))
    return (density_rate, acceleration, time_step)


def solution(mesh):
    return jax.shard_map(
        per_device,
        mesh=mesh,
        in_specs=(
            P(None, ("orb", "wall")),
            P(None, ("orb", "wall")),
            P(("orb", "wall"), None),
            P(None, ("orb", "wall")),
            P(("orb", "wall")),
            P(("orb", "wall"), None),
        ),
        out_specs=(P(("orb", "wall")), P(None, ("orb", "wall")), P()),
        check_vma=False,
    )
```

profile of v0, /device:TPU:1, one launch (start us, length us, event | category | flops | bytes accessed | tf_op | source)
XLA Modules:
  0.0 213.7 jit_solution(5112951119415399424)
XLA Ops:
  2.8 4.0 %collective-permute-start.12 = (f32[4,128]{1,0:T(4,128)S(1)}, f32[4,128]{1,0:T(4,128)S(1)}, u32[]{:S(2)}, u32[]{:S(2)}) collective-permute-start(f32[4,128]{1,0:T(4,128)S(1)} %get-tuple-element.229), channel_id=1, source_target_pairs={{0,1},{1,2},{2,3},{4,5},{5,6},{6,7},{8,9},{9,10},{10,11},{12,13},{... | collective-permute-start | bytes 6152 | tf_op jit(solution)/shard_map/ppermute | solution.py:30
  8.9 1.5 gather_fusion.2
  11.4 1.6 collective-permute-start.1
  16.4 3.0 %collective-permute-start.4 = (f32[6,8,128]{2,1,0:T(8,128)S(1)}, f32[6,8,128]{2,1,0:T(8,128)S(1)}, u32[]{:S(2)}, u32[]{:S(2)}) collective-permute-start(f32[6,8,128]{2,1,0:T(8,128)S(1)} %get-tuple-element.225), channel_id=1, source_target_pairs={{0,16},{4,20},{8,24},{12,28},{16,0},{20,4},{24,8},{28,12},{32,48},... | collective-permute-start | bytes 73736 | tf_op jit(solution)/shard_map/ppermute | solution.py:22
  19.4 1.6 collective-permute-start.3
  21.2 2.3 %collective-permute-start.8 = (f32[6,8,128]{2,1,0:T(8,128)S(1)}, f32[6,8,128]{2,1,0:T(8,128)S(1)}, u32[]{:S(2)}, u32[]{:S(2)}) collective-permute-start(f32[6,8,128]{2,1,0:T(8,128)S(1)} %collective-permute-done.7), channel_id=1, source_target_pairs={{0,16},{4,20},{8,24},{12,28},{16,0},{20,4},{24,8},{28,12},{32,48},... | collective-permute-start | bytes 73736 | tf_op jit(solution)/shard_map/ppermute | solution.py:22
  23.5 3.1 %collective-permute-done.10 = f32[6,8,128]{2,1,0:T(8,128)S(1)} collective-permute-done((f32[6,8,128]{2,1,0:T(8,128)S(1)}, f32[6,8,128]{2,1,0:T(8,128)S(1)}, u32[]{:S(2)}, u32[]{:S(2)}) %collective-permute-start.10) | collective-permute-done | bytes 24608 | tf_op jit(solution)/shard_map/ppermute | solution.py:22
  26.7 3.5 %collective-permute-done.11 = f32[6,8,128]{2,1,0:T(8,128)S(1)} collective-permute-done((f32[6,8,128]{2,1,0:T(8,128)S(1)}, f32[6,8,128]{2,1,0:T(8,128)S(1)}, u32[]{:S(2)}, u32[]{:S(2)}) %collective-permute-start.11) | collective-permute-done | bytes 24608 | tf_op jit(solution)/shard_map/ppermute | solution.py:22
  31.1 100.0 %while.16 = (s32[]{:T(128)}, f32[12,2,128]{2,1,0:T(2,128)S(1)}, f32[12,2,3,128]{3,2,1,0:T(4,128)S(1)}, s32[12,2,14]{2,1,0:T(2,128)S(1)}, f32[66,8,128]{2,1,0:T(8...) while((s32[]{:T(128)}, f32[12,2,128]{2,1,0:T(2,128)S(1)}, ...), condition=%wide.region_9.10_spmd.clone, body=%wide.region_0.9_spmd.sunk.clone.sunk | while | flops 28604780 | bytes 15659557 | solution.py:116
  34.1 2.3 %add_multiply_fusion.4 = (f32[2,14,128,128]{3,2,1,0:T(8,128)S(1)}, f32[2,128]{1,0:T(2,128)S(1)}) fusion(f32[2,14,128,128]{3,2,1,0:T(8,128)S(1)} %get-tuple-element.301, f32[2,14,128,128]{3,2,1,0:T(8,128)S(1)} %get-tuple-element.302, f32[2,14,128]{2,1,0:T(8,128)S(1)} %copy.76, f32[2,128]{1,0:T(2,128)S(1)} %slice_bitcast_fusion.2, ...), kind=kLoop, calls=%fused_computation.13.clone.1 | loop fusion | flops 11468544 | bytes 5551104 | tf_op jit(solution)/shard_map/while/body/eval_jaxpr/vmap()/mul | solution.py:70
  40.9 1.5 fusion.32
  42.5 2.3 %add_multiply_fusion.4 = (f32[2,14,128,128]{3,2,1,0:T(8,128)S(1)}, f32[2,128]{1,0:T(2,128)S(1)}) fusion(f32[2,14,128,128]{3,2,1,0:T(8,128)S(1)} %get-tuple-element.301, f32[2,14,128,128]{3,2,1,0:T(8,128)S(1)} %get-tuple-element.302, f32[2,14,128]{2,1,0:T(8,128)S(1)} %copy.76, f32[2,128]{1,0:T(2,128)S(1)} %slice_bitcast_fusion.2, ...), kind=kLoop, calls=%fused_computation.13.clone.1 | loop fusion | flops 11468544 | bytes 5551104 | tf_op jit(solution)/shard_map/while/body/eval_jaxpr/vmap()/mul | solution.py:70
  49.2 1.5 fusion.32
  50.8 2.3 %add_multiply_fusion.4 = (f32[2,14,128,128]{3,2,1,0:T(8,128)S(1)}, f32[2,128]{1,0:T(2,128)S(1)}) fusion(f32[2,14,128,128]{3,2,1,0:T(8,128)S(1)} %get-tuple-element.301, f32[2,14,128,128]{3,2,1,0:T(8,128)S(1)} %get-tuple-element.302, f32[2,14,128]{2,1,0:T(8,128)S(1)} %copy.76, f32[2,128]{1,0:T(2,128)S(1)} %slice_bitcast_fusion.2, ...), kind=kLoop, calls=%fused_computation.13.clone.1 | loop fusion | flops 11468544 | bytes 5551104 | tf_op jit(solution)/shard_map/while/body/eval_jaxpr/vmap()/mul | solution.py:70
  59.1 2.3 %add_multiply_fusion.4 = (f32[2,14,128,128]{3,2,1,0:T(8,128)S(1)}, f32[2,128]{1,0:T(2,128)S(1)}) fusion(f32[2,14,128,128]{3,2,1,0:T(8,128)S(1)} %get-tuple-element.301, f32[2,14,128,128]{3,2,1,0:T(8,128)S(1)} %get-tuple-element.302, f32[2,14,128]{2,1,0:T(8,128)S(1)} %copy.76, f32[2,128]{1,0:T(2,128)S(1)} %slice_bitcast_fusion.2, ...), kind=kLoop, calls=%fused_computation.13.clone.1 | loop fusion | flops 11468544 | bytes 5551104 | tf_op jit(solution)/shard_map/while/body/eval_jaxpr/vmap()/mul | solution.py:70
  67.5 2.3 %add_multiply_fusion.4 = (f32[2,14,128,128]{3,2,1,0:T(8,128)S(1)}, f32[2,128]{1,0:T(2,128)S(1)}) fusion(f32[2,14,128,128]{3,2,1,0:T(8,128)S(1)} %get-tuple-element.301, f32[2,14,128,128]{3,2,1,0:T(8,128)S(1)} %get-tuple-element.302, f32[2,14,128]{2,1,0:T(8,128)S(1)} %copy.76, f32[2,128]{1,0:T(2,128)S(1)} %slice_bitcast_fusion.2, ...), kind=kLoop, calls=%fused_computation.13.clone.1 | loop fusion | flops 11468544 | bytes 5551104 | tf_op jit(solution)/shard_map/while/body/eval_jaxpr/vmap()/mul | solution.py:70
  75.8 2.3 %add_multiply_fusion.4 = (f32[2,14,128,128]{3,2,1,0:T(8,128)S(1)}, f32[2,128]{1,0:T(2,128)S(1)}) fusion(f32[2,14,128,128]{3,2,1,0:T(8,128)S(1)} %get-tuple-element.301, f32[2,14,128,128]{3,2,1,0:T(8,128)S(1)} %get-tuple-element.302, f32[2,14,128]{2,1,0:T(8,128)S(1)} %copy.76, f32[2,128]{1,0:T(2,128)S(1)} %slice_bitcast_fusion.2, ...), kind=kLoop, calls=%fused_computation.13.clone.1 | loop fusion | flops 11468544 | bytes 5551104 | tf_op jit(solution)/shard_map/while/body/eval_jaxpr/vmap()/mul | solution.py:70
  84.1 2.3 %add_multiply_fusion.4 = (f32[2,14,128,128]{3,2,1,0:T(8,128)S(1)}, f32[2,128]{1,0:T(2,128)S(1)}) fusion(f32[2,14,128,128]{3,2,1,0:T(8,128)S(1)} %get-tuple-element.301, f32[2,14,128,128]{3,2,1,0:T(8,128)S(1)} %get-tuple-element.302, f32[2,14,128]{2,1,0:T(8,128)S(1)} %copy.76, f32[2,128]{1,0:T(2,128)S(1)} %slice_bitcast_fusion.2, ...), kind=kLoop, calls=%fused_computation.13.clone.1 | loop fusion | flops 11468544 | bytes 5551104 | tf_op jit(solution)/shard_map/while/body/eval_jaxpr/vmap()/mul | solution.py:70
  92.5 2.3 %add_multiply_fusion.4 = (f32[2,14,128,128]{3,2,1,0:T(8,128)S(1)}, f32[2,128]{1,0:T(2,128)S(1)}) fusion(f32[2,14,128,128]{3,2,1,0:T(8,128)S(1)} %get-tuple-element.301, f32[2,14,128,128]{3,2,1,0:T(8,128)S(1)} %get-tuple-element.302, f32[2,14,128]{2,1,0:T(8,128)S(1)} %copy.76, f32[2,128]{1,0:T(2,128)S(1)} %slice_bitcast_fusion.2, ...), kind=kLoop, calls=%fused_computation.13.clone.1 | loop fusion | flops 11468544 | bytes 5551104 | tf_op jit(solution)/shard_map/while/body/eval_jaxpr/vmap()/mul | solution.py:70
  100.8 2.3 %add_multiply_fusion.4 = (f32[2,14,128,128]{3,2,1,0:T(8,128)S(1)}, f32[2,128]{1,0:T(2,128)S(1)}) fusion(f32[2,14,128,128]{3,2,1,0:T(8,128)S(1)} %get-tuple-element.301, f32[2,14,128,128]{3,2,1,0:T(8,128)S(1)} %get-tuple-element.302, f32[2,14,128]{2,1,0:T(8,128)S(1)} %copy.76, f32[2,128]{1,0:T(2,128)S(1)} %slice_bitcast_fusion.2, ...), kind=kLoop, calls=%fused_computation.13.clone.1 | loop fusion | flops 11468544 | bytes 5551104 | tf_op jit(solution)/shard_map/while/body/eval_jaxpr/vmap()/mul | solution.py:70
  109.1 2.3 %add_multiply_fusion.4 = (f32[2,14,128,128]{3,2,1,0:T(8,128)S(1)}, f32[2,128]{1,0:T(2,128)S(1)}) fusion(f32[2,14,128,128]{3,2,1,0:T(8,128)S(1)} %get-tuple-element.301, f32[2,14,128,128]{3,2,1,0:T(8,128)S(1)} %get-tuple-element.302, f32[2,14,128]{2,1,0:T(8,128)S(1)} %copy.76, f32[2,128]{1,0:T(2,128)S(1)} %slice_bitcast_fusion.2, ...), kind=kLoop, calls=%fused_computation.13.clone.1 | loop fusion | flops 11468544 | bytes 5551104 | tf_op jit(solution)/shard_map/while/body/eval_jaxpr/vmap()/mul | solution.py:70
  117.5 2.3 %add_multiply_fusion.4 = (f32[2,14,128,128]{3,2,1,0:T(8,128)S(1)}, f32[2,128]{1,0:T(2,128)S(1)}) fusion(f32[2,14,128,128]{3,2,1,0:T(8,128)S(1)} %get-tuple-element.301, f32[2,14,128,128]{3,2,1,0:T(8,128)S(1)} %get-tuple-element.302, f32[2,14,128]{2,1,0:T(8,128)S(1)} %copy.76, f32[2,128]{1,0:T(2,128)S(1)} %slice_bitcast_fusion.2, ...), kind=kLoop, calls=%fused_computation.13.clone.1 | loop fusion | flops 11468544 | bytes 5551104 | tf_op jit(solution)/shard_map/while/body/eval_jaxpr/vmap()/mul | solution.py:70
  125.8 2.3 %add_multiply_fusion.4 = (f32[2,14,128,128]{3,2,1,0:T(8,128)S(1)}, f32[2,128]{1,0:T(2,128)S(1)}) fusion(f32[2,14,128,128]{3,2,1,0:T(8,128)S(1)} %get-tuple-element.301, f32[2,14,128,128]{3,2,1,0:T(8,128)S(1)} %get-tuple-element.302, f32[2,14,128]{2,1,0:T(8,128)S(1)} %copy.76, f32[2,128]{1,0:T(2,128)S(1)} %slice_bitcast_fusion.2, ...), kind=kLoop, calls=%fused_computation.13.clone.1 | loop fusion | flops 11468544 | bytes 5551104 | tf_op jit(solution)/shard_map/while/body/eval_jaxpr/vmap()/mul | solution.py:70
  132.4 79.5 %pmax.7 = f32[]{:T(128)} all-reduce(f32[]{:T(128)} %sqrt_reduce_fusion), channel_id=1, replica_groups=mesh['orb'=64,'wall'=4] {'orb','wall'}, use_global_device_ids=true, to_apply=%region_12.13 | all-reduce | flops 1 | bytes 8 | tf_op jit(solution)/shard_map/pmax | solution.py:122
  (429 shorter events, 78.3 us)
Async XLA Ops:
  2.8 12.2 %collective-permute-start.12 = (f32[4,128]{1,0:T(4,128)S(1)}, f32[4,128]{1,0:T(4,128)S(1)}, u32[]{:S(2)}, u32[]{:S(2)}) collective-permute-start(f32[4,128]{1,0:T(4,128)S(1)} %get-tuple-element.229), channel_id=1, source_target_pairs={{0,1},{1,2},{2,3},{4,5},{5,6},{6,7},{8,9},{9,10},{10,11},{12,13},{... | collective-permute-start | bytes 6152 | tf_op jit(solution)/shard_map/ppermute | solution.py:30
  6.8 8.3 %collective-permute-start.13 = (f32[4,128]{1,0:T(4,128)S(1)}, f32[4,128]{1,0:T(4,128)S(1)}, u32[]{:S(2)}, u32[]{:S(2)}) collective-permute-start(f32[4,128]{1,0:T(4,128)S(1)} %get-tuple-element.230), channel_id=1, source_target_pairs={{1,0},{2,1},{3,2},{5,4},{6,5},{7,6},{9,8},{10,9},{11,10},{13,12},{... | collective-permute-start | bytes 6152 | tf_op jit(solution)/shard_map/ppermute | solution.py:33
  10.4 5.5 %collective-permute-start = (f32[6,8,128]{2,1,0:T(8,128)S(1)}, f32[6,8,128]{2,1,0:T(8,128)S(1)}, u32[]{:S(2)}, u32[]{:S(2)}) collective-permute-start(f32[6,8,128]{2,1,0:T(8,128)S(1)} %get-tuple-element.228), channel_id=1, source_target_pairs={{0,4},{4,0},{8,12},{12,8},{16,20},{20,16},{24,28},{28,24},{32,36},... | collective-permute-start | bytes 73736 | tf_op jit(solution)/shard_map/ppermute | solution.py:22
  11.4 5.0 %collective-permute-start.1 = (f32[6,8,128]{2,1,0:T(8,128)S(1)}, f32[6,8,128]{2,1,0:T(8,128)S(1)}, u32[]{:S(2)}, u32[]{:S(2)}) collective-permute-start(f32[6,8,128]{2,1,0:T(8,128)S(1)} %get-tuple-element.227), channel_id=1, source_target_pairs={{0,8},{4,12},{8,0},{12,4},{16,24},{20,28},{24,16},{28,20},{32,40},... | collective-permute-start | bytes 73736 | tf_op jit(solution)/shard_map/ppermute | solution.py:22
  13.1 6.4 %collective-permute-start.2 = (f32[6,8,128]{2,1,0:T(8,128)S(1)}, f32[6,8,128]{2,1,0:T(8,128)S(1)}, u32[]{:S(2)}, u32[]{:S(2)}) collective-permute-start(f32[6,8,128]{2,1,0:T(8,128)S(1)} %get-tuple-element.226), channel_id=1, source_target_pairs={{0,4},{4,0},{8,12},{12,8},{16,20},{20,16},{24,28},{28,24},{32,36},... | collective-permute-start | bytes 73736 | tf_op jit(solution)/shard_map/ppermute | solution.py:22
  15.0 6.1 %collective-permute-start.5 = (f32[6,8,128]{2,1,0:T(8,128)S(1)}, f32[6,8,128]{2,1,0:T(8,128)S(1)}, u32[]{:S(2)}, u32[]{:S(2)}) collective-permute-start(f32[6,8,128]{2,1,0:T(8,128)S(1)} %get-tuple-element.224), channel_id=1, source_target_pairs={{0,4},{4,0},{8,12},{12,8},{16,20},{20,16},{24,28},{28,24},{32,36},... | collective-permute-start | bytes 73736 | tf_op jit(solution)/shard_map/ppermute | solution.py:22
  15.1 6.1 %collective-permute-start.7 = (f32[6,8,128]{2,1,0:T(8,128)S(1)}, f32[6,8,128]{2,1,0:T(8,128)S(1)}, u32[]{:S(2)}, u32[]{:S(2)}) collective-permute-start(f32[6,8,128]{2,1,0:T(8,128)S(1)} %get-tuple-element.223), channel_id=1, source_target_pairs={{0,8},{4,12},{8,0},{12,4},{16,24},{20,28},{24,16},{28,20},{32,40},... | collective-permute-start | bytes 73736 | tf_op jit(solution)/shard_map/ppermute | solution.py:22
  15.9 7.6 %collective-permute-start.9 = (f32[6,8,128]{2,1,0:T(8,128)S(1)}, f32[6,8,128]{2,1,0:T(8,128)S(1)}, u32[]{:S(2)}, u32[]{:S(2)}) collective-permute-start(f32[6,8,128]{2,1,0:T(8,128)S(1)} %get-tuple-element.222), channel_id=1, source_target_pairs={{0,4},{4,0},{8,12},{12,8},{16,20},{20,16},{24,28},{28,24},{32,36},... | collective-permute-start | bytes 73736 | tf_op jit(solution)/shard_map/ppermute | solution.py:22
  16.4 10.2 %collective-permute-start.4 = (f32[6,8,128]{2,1,0:T(8,128)S(1)}, f32[6,8,128]{2,1,0:T(8,128)S(1)}, u32[]{:S(2)}, u32[]{:S(2)}) collective-permute-start(f32[6,8,128]{2,1,0:T(8,128)S(1)} %get-tuple-element.225), channel_id=1, source_target_pairs={{0,16},{4,20},{8,24},{12,28},{16,0},{20,4},{24,8},{28,12},{32,48},... | collective-permute-start | bytes 73736 | tf_op jit(solution)/shard_map/ppermute | solution.py:22
  19.4 7.2 %collective-permute-start.3 = (f32[6,8,128]{2,1,0:T(8,128)S(1)}, f32[6,8,128]{2,1,0:T(8,128)S(1)}, u32[]{:S(2)}, u32[]{:S(2)}) collective-permute-start(f32[6,8,128]{2,1,0:T(8,128)S(1)} %collective-permute-done.2), channel_id=1, source_target_pairs={{0,8},{4,12},{8,0},{12,4},{16,24},{20,28},{24,16},{28,20},{32,40},... | collective-permute-start | bytes 73736 | tf_op jit(solution)/shard_map/ppermute | solution.py:22
  21.1 5.6 %collective-permute-start.6 = (f32[6,8,128]{2,1,0:T(8,128)S(1)}, f32[6,8,128]{2,1,0:T(8,128)S(1)}, u32[]{:S(2)}, u32[]{:S(2)}) collective-permute-start(f32[6,8,128]{2,1,0:T(8,128)S(1)} %collective-permute-done.5), channel_id=1, source_target_pairs={{0,16},{4,20},{8,24},{12,28},{16,0},{20,4},{24,8},{28,12},{32,48},... | collective-permute-start | bytes 73736 | tf_op jit(solution)/shard_map/ppermute | solution.py:22
  21.2 5.5 %collective-permute-start.8 = (f32[6,8,128]{2,1,0:T(8,128)S(1)}, f32[6,8,128]{2,1,0:T(8,128)S(1)}, u32[]{:S(2)}, u32[]{:S(2)}) collective-permute-start(f32[6,8,128]{2,1,0:T(8,128)S(1)} %collective-permute-done.7), channel_id=1, source_target_pairs={{0,16},{4,20},{8,24},{12,28},{16,0},{20,4},{24,8},{28,12},{32,48},... | collective-permute-start | bytes 73736 | tf_op jit(solution)/shard_map/ppermute | solution.py:22
  23.4 3.1 %collective-permute-start.10 = (f32[6,8,128]{2,1,0:T(8,128)S(1)}, f32[6,8,128]{2,1,0:T(8,128)S(1)}, u32[]{:S(2)}, u32[]{:S(2)}) collective-permute-start(f32[6,8,128]{2,1,0:T(8,128)S(1)} %collective-permute-done.9), channel_id=1, source_target_pairs={{0,8},{4,12},{8,0},{12,4},{16,24},{20,28},{24,16},{28,20},{32,40},... | collective-permute-start | bytes 73736 | tf_op jit(solution)/shard_map/ppermute | solution.py:22
  26.6 3.6 %collective-permute-start.11 = (f32[6,8,128]{2,1,0:T(8,128)S(1)}, f32[6,8,128]{2,1,0:T(8,128)S(1)}, u32[]{:S(2)}, u32[]{:S(2)}) collective-permute-start(f32[6,8,128]{2,1,0:T(8,128)S(1)} %collective-permute-done.10), channel_id=1, source_target_pairs={{0,16},{4,20},{8,24},{12,28},{16,0},{20,4},{24,8},{28,12},{32,48},... | collective-permute-start | bytes 73736 | tf_op jit(solution)/shard_map/ppermute | solution.py:22
  37.2 1.7 copy-start
  45.6 1.7 copy-start
  53.9 1.7 copy-start
  62.2 1.7 copy-start
  70.6 1.7 copy-start
  78.9 1.7 copy-start
  87.2 1.7 copy-start
  95.6 1.7 copy-start
  103.9 1.7 copy-start
  131.1 81.5 %copy-start.1 = (f32[12,2,128]{2,1,0:T(2,128)}, f32[12,2,128]{2,1,0:T(2,128)S(1)}, u32[]{:S(2)}) copy-start(f32[12,2,128]{2,1,0:T(2,128)S(1)} %get-tuple-element.152) | copy-start | bytes 36868
  (3 other events, 5.2 us)
where the time goes:
time: 215 us; the launch traced here: 214 us
  blocking collectives  79.5 us (37%)
  other arithmetic  77.9 us (36%)
  local copies, waits for them, and re-layouts  29.1 us (14%)
  starting transfers between devices  16.2 us (8%)
  waiting for transfers between devices  6.58 us (3%)
  between operations  2.64 us (1%)
    pmax x1, blocking collectives, per_device(): peak = lax.pmax(local_peak, ('orb', 'wall'))  79.5 us
    mul x12, other arithmetic, block_terms(): weight = mass_row * (press_term * grad_scale + cohesion * pull)  27.9 us
    reduce_sum x24, other arithmetic, kernel_parts(): dist_sq = jnp.sum(offset * offset, axis=1)  20 us
    gather x24, local copies, waits for them, and re-layouts, per_block(): return block_terms(target, candidates[pair_row], wall_cands[wall_row])  13.8 us
    ppermute x12, starting transfers between devices, swapped(): lax.ppermute(shard, axis, [(i, i ^ 1 << bit) for i in range(lax.axis_size...  10.9 us
    reduce_sum x12, other arithmetic, block_terms(): fluid_force = -jnp.sum(weight[:, None] * offset, axis=(0, 3))  9.01 us
    dynamic_slice x24, local copies, waits for them, and re-layouts, per_device(): lax.map(per_group, (grouped(own_blocks), grouped(pair_list), grouped(wall...  8.52 us
    ppermute x12, waiting for transfers between devices, swapped(): lax.ppermute(shard, axis, [(i, i ^ 1 << bit) for i in range(lax.axis_size...  6.57 us
  transfers between devices with their start and end apart: 14, of which 2 were waited for; matrix products, arithmetic and copies ran while one was open for 2% of the time, Pallas kernels for 0%

commit v1 on v0

v1 whole, which is shorter than its diff:
```python
import jax
import jax.numpy as jnp
from jax import lax
from jax.experimental import pallas as pl
from jax.experimental.pallas import tpu as pltpu
from jax.sharding import PartitionSpec as P

NB = 24
K = 14
KW = 4
GH = 6
WB = 6
EB = 1
NC = NB + 7 * GH
NW = WB + 2 * EB
LN = 128

smoothing = 0.1
support = 0.3
kernel_norm = 21.0 / (2.0 * 3.141592653589793 * support**3)
grad_coeff = -20.0 / support**2 * kernel_norm
tait_coeff = 25.0 / 7.0
visc_coeff = 0.05
cohesion = 2000.0
adhesion = 2000.0
gravity = 9.81
courant = 0.25

center = 0.3
inv_support = 1.0 / support
eps_scaled = 0.0001 / support**2
visc_scaled = visc_coeff * -grad_coeff / support

F32 = jnp.float32
BF16 = jnp.bfloat16


def split(value, terms):
    parts = []
    for _ in range(terms - 1):
        high = value.astype(BF16).astype(F32)
        parts.append(high)
        value = value - high
    parts.append(value.astype(BF16).astype(F32))
    return parts


def pressure_of(density):
    return tait_coeff * (density**7 - 1.0)


def dot3(a, b):
    return a[0] * b[0] + a[1] * b[1] + a[2] * b[2]


CROSS = ((0, 0), (0, 1), (0, 2), (1, 0), (1, 1), (2, 0))


def source_rows(y, v, rho_half):
    ys = [split(c, 3) for c in y]
    norm = split(dot3(y, y), 3)
    one = jnp.ones_like(y[0])
    rows = []
    for c in range(3):
        rows += [ys[c][j] for j, _ in CROSS]
    rows += [one] * 3
    rows += norm
    if v is None:
        return rows
    vs = [split(c, 2) for c in v]
    vt = [c[0] + c[1] for c in vs]
    for c in range(3):
        rows += [vs[c][0], vs[c][0], vs[c][0], vs[c][1], vs[c][1]]
    rows += split(dot3(vt, y), 3)
    rows += [norm[0], norm[0], norm[1]]
    rows += split(rho_half * dot3(y, y), 3)
    hs = split(rho_half, 3)
    rows += [hs[j] for j, _ in CROSS]
    for c in range(3):
        hy = split(rho_half * y[c], 3)
        rows += [hy[j] for j, _ in CROSS]
    return rows


def target_rows(y, v, rho_half):
    ys = [split(c, 3) for c in y]
    vs = [split(c, 2) for c in v]
    vt = [c[0] + c[1] for c in vs]
    sq = dot3(y, y)
    norm = split(sq, 3)
    reach = sq + eps_scaled
    vy = split(dot3(vt, y), 3)
    hs = split(rho_half, 3)
    hn = split(rho_half * reach, 3)
    rs = split(reach, 3)
    one = jnp.ones_like(y[0])
    zero = jnp.zeros_like(y[0])
    rows = []
    for c in range(3):
        hy = split(rho_half * y[c], 3)
        for _, i in CROSS:
            approach = -vs[c][i] if i < 2 else zero
            rows.append((-2.0 * ys[c][i], approach, -2.0 * hy[i]))
    for i in range(3):
        rows.append((norm[i], vy[i], hn[i]))
    for i in range(3):
        rows.append((one, zero, hs[0]))
    for c in range(3):
        for i in (0, 1, 2, 0, 1):
            rows.append((zero, -ys[c][i], zero))
    rows += [(zero, one, zero)] * 3
    rows += [(zero, zero, hs[1]), (zero, zero, hs[2]), (zero, zero, hs[1])]
    rows += [(zero, zero, one)] * 3
    for _, i in CROSS:
        rows.append((zero, zero, rs[i]))
    for c in range(3):
        for _, i in CROSS:
            rows.append((zero, zero, -2.0 * ys[c][i]))
    return rows


KR = 72
KWALL = 24


def column_rows(quantities):
    parts = [split(q, 2) for q in quantities]
    return [p[0] for p in parts], [p[1] for p in parts]


def falloff_of(dist_sq):
    dist_sq = jnp.maximum(dist_sq, 1e-30)
    s = jnp.maximum(1.0 - dist_sq * lax.rsqrt(dist_sq), 0.0)
    return s, s * s * s


def two_terms(value):
    high = value.astype(BF16)
    return high, (value - high.astype(F32)).astype(BF16)


def pair_kernel(
    pair_ref, wpair_ref, own_ref, ghost_ref, wall_ref, rate_ref, accel_ref, peak_ref,
    cand, wcand, jf32, if32, wf32, cl32, wc32, jf, tf, wf, cl, wc, sums, wsums,
):
    for b in range(NB):
        cand[8 * b : 8 * b + 8, :] = own_ref[:, LN * b : LN * b + LN]
    cand[8 * NB :, :] = ghost_ref[...]
    for b in range(NW):
        wcand[4 * b : 4 * b + 4, :] = wall_ref[:, LN * b : LN * b + LN]

    state = [cand[pl.ds(r, NC, stride=8), :] for r in range(8)]
    y = [(state[c] - center) * inv_support for c in range(3)]
    v = state[3:6]
    rho, mass = state[6], state[7]
    rho_half = (0.5 / visc_scaled) * rho
    push = pressure_of(rho) / (rho * rho)

    rows = source_rows(y, v, rho_half)
    assert len(rows) == KR
    for k, row in enumerate(rows):
        jf32[pl.ds(k, NC, stride=KR), :] = row
    vt = v
    cols = [mass] + [mass * c for c in y] + [mass * c for c in vt]
    cols += [mass * dot3(vt, y), mass * push] + [mass * push * c for c in y]
    high, low = column_rows(cols)
    cl32[...] = jnp.zeros_like(cl32)
    for k in range(12):
        cl32[pl.ds(k, NC, stride=32), :] = high[k]
        cl32[pl.ds(16 + k, NC, stride=32), :] = low[k]

    ty = [c[:NB] for c in y]
    tv = [c[:NB] for c in v]
    weights = target_rows(ty, tv, rho_half[:NB])
    assert len(weights) == KR
    for k, row in enumerate(weights):
        for part in range(3):
            if32[part, pl.ds(k, NB, stride=KR), :] = row[part]

    wstate = [wcand[pl.ds(r, NW, stride=4), :] for r in range(4)]
    wy = [(wstate[c] - center) * inv_support for c in range(3)]
    wrows = source_rows(wy, None, None)
    assert len(wrows) == KWALL
    for k, row in enumerate(wrows):
        wf32[pl.ds(k, NW, stride=KWALL), :] = row
    whigh, wlow = column_rows([wstate[3]] + [wstate[3] * c for c in wy])
    wc32[...] = jnp.zeros_like(wc32)
    for k in range(4):
        wc32[pl.ds(k, NW, stride=16), :] = whigh[k]
        wc32[pl.ds(8 + k, NW, stride=16), :] = wlow[k]

    def build_source(b, carry):
        rows = jf32[pl.ds(b * KR, KR), :]
        rows = jnp.concatenate([rows, jnp.zeros((LN - KR, LN), F32)], axis=0)
        jf[b] = rows.T.astype(BF16)
        c = cl32[pl.ds(b * 32, 32), :].astype(BF16)
        cl[b] = jnp.concatenate([c, c], axis=1)
        return carry

    lax.fori_loop(0, NC, build_source, 0, unroll=6)

    def build_target(b, carry):
        for part in range(3):
            rows = if32[part, pl.ds(b * KR, KR), :]
            rows = jnp.concatenate([rows, jnp.zeros((LN - KR, LN), F32)], axis=0)
            tf[b, :, LN * part : LN * part + LN] = rows.astype(BF16)
        return carry

    lax.fori_loop(0, NB, build_target, 0)

    def build_wall(b, carry):
        rows = wf32[pl.ds(b * KWALL, KWALL), :]
        rows = jnp.concatenate([rows, jnp.zeros((LN - KWALL, LN), F32)], axis=0)
        wf[b] = rows.T.astype(BF16)
        c = wc32[pl.ds(b * 16, 16), :].astype(BF16)
        wc[b] = jnp.concatenate([c, c], axis=1)
        return carry

    lax.fori_loop(0, NW, build_wall, 0)

    def block(b, carry):
        weights = tf[b]
        total = jnp.zeros((32, 2 * LN), F32)
        for k in range(K):
            j = pair_ref[b, k]
            geo = jnp.dot(jf[j], weights, preferred_element_type=F32)
            s, cubed = falloff_of(geo[:, :LN])
            root = lax.rsqrt(geo[:, 2 * LN :])
            drag = jnp.minimum(geo[:, LN : 2 * LN], 0.0) * (root * root)
            pull = cubed * (drag + (3.0 * cohesion - 4.0 * cohesion * s))
            sh, sl = two_terms(cubed)
            uh, ul = two_terms(pull)
            mat = jnp.concatenate(
                [jnp.concatenate([sh, uh], axis=1), jnp.concatenate([sl, ul], axis=1)], axis=0
            )
            total += jnp.dot(cl[j], mat, preferred_element_type=F32)
        sums[b] = total[:16] + total[16:]
        wtotal = jnp.zeros((16, 2 * LN), F32)
        for k in range(KW):
            j = wpair_ref[b, k]
            geo = jnp.dot(wf[j], weights[:, :LN], preferred_element_type=F32)
            s, cubed = falloff_of(geo)
            pull = cubed * (3.0 * adhesion - 4.0 * adhesion * s)
            sh, sl = two_terms(cubed)
            uh, ul = two_terms(pull)
            mat = jnp.concatenate(
                [jnp.concatenate([sh, uh], axis=1), jnp.concatenate([sl, ul], axis=1)], axis=0
            )
            wtotal += jnp.dot(wc[j], mat, preferred_element_type=F32)
        wsums[b] = wtotal[:8] + wtotal[8:]
        return carry

    lax.fori_loop(0, NB, block, 0)

    def take(ref, row, lane):
        return ref[:, row, lane : lane + LN]

    spart = [take(sums, r, 0) for r in range(12)]
    upart = [take(sums, r, LN) for r in range(4)]
    wspart = [take(wsums, r, 0) for r in range(4)]
    wupart = [take(wsums, r, LN) for r in range(4)]
    own_push = push[:NB]
    rate = (
        dot3(tv, ty) * (spart[0] + wspart[0])
        - dot3(tv, [spart[1 + c] + wspart[1 + c] for c in range(3)])
        - dot3(spart[4:7], ty)
        + spart[7]
    )
    rate_ref[...] = (grad_coeff * support) * rate
    square = jnp.zeros((NB, LN), F32)
    for c in range(3):
        pressed = own_push * (
            ty[c] * (spart[0] + 2.0 * wspart[0]) - (spart[1 + c] + 2.0 * wspart[1 + c])
        )
        pressed += ty[c] * spart[8] - spart[9 + c]
        pulled = ty[c] * (upart[0] + wupart[0]) - (upart[1 + c] + wupart[1 + c])
        force = (-grad_coeff * support) * pressed - support * pulled
        if c == 2:
            force = force - gravity
        square += force * force
        for b in range(NB):
            accel_ref[c : c + 1, LN * b : LN * b + LN] = force[b : b + 1]
    peak = jnp.max(jnp.sqrt(square), axis=0, keepdims=True)
    peak_ref[...] = jnp.broadcast_to(jnp.max(peak, axis=1, keepdims=True), (8, LN))


def pair_forces(pairs, wpairs, own, ghosts, walls, **kw):
    vmem = pl.BlockSpec(memory_space=pltpu.VMEM)
    smem = pl.BlockSpec(memory_space=pltpu.SMEM)
    return pl.pallas_call(
        pair_kernel,
        name="pair_forces",
        out_shape=(
            jax.ShapeDtypeStruct((NB, LN), F32),
            jax.ShapeDtypeStruct((3, NB * LN), F32),
            jax.ShapeDtypeStruct((8, LN), F32),
        ),
        in_specs=[smem, smem, vmem, vmem, vmem],
        out_specs=(vmem, vmem, vmem),
        scratch_shapes=[
            pltpu.VMEM((NC * 8, LN), F32),
            pltpu.VMEM((NW * 4, LN), F32),
            pltpu.VMEM((NC * KR, LN), F32),
            pltpu.VMEM((3, NB * KR, LN), F32),
            pltpu.VMEM((NW * KWALL, LN), F32),
            pltpu.VMEM((NC * 32, LN), F32),
            pltpu.VMEM((NW * 16, LN), F32),
            pltpu.VMEM((NC, LN, LN), BF16),
            pltpu.VMEM((NB, LN, 3 * LN), BF16),
            pltpu.VMEM((NW, LN, LN), BF16),
            pltpu.VMEM((NC, 32, 2 * LN), BF16),
            pltpu.VMEM((NW, 16, 2 * LN), BF16),
            pltpu.VMEM((NB, 16, 2 * LN), F32),
            pltpu.VMEM((NB, 8, 2 * LN), F32),
        ],
        **kw,
    )(pairs, wpairs, own, ghosts, walls)


def padded(block, axis, width):
    count = lax.axis_size(axis)
    forward = [(i, i + 1) for i in range(count - 1)]
    backward = [(target, source) for source, target in forward]
    low = lax.ppermute(block[:, block.shape[1] - width :], axis, forward)
    high = lax.ppermute(block[:, :width], axis, backward)
    return jnp.concatenate([low, block, high], axis=1)


def per_device(fluid_state, ghost_list, pair_list, wall_state, wall_count, wall_pairs):
    own_blocks = jnp.transpose(fluid_state.reshape(8, NB, LN), (1, 0, 2))
    outgoing = own_blocks[ghost_list]
    size = lax.axis_size("orb")
    arrived = [
        lax.ppermute(outgoing[q - 1], "orb", [(i, i ^ q) for i in range(size)]) for q in range(1, 8)
    ]
    ghosts = jnp.concatenate(arrived).reshape(-1, LN)
    alive = (jnp.arange(LN, dtype=jnp.int32)[None, :] < wall_count[:, None]).astype(F32).reshape(-1)
    wall_live = jnp.concatenate([wall_state[0:3], wall_state[3:4] * alive[None, :]], axis=0)
    walls = padded(wall_live, "wall", EB * LN)
    rates, acceleration, peak = pair_forces(pair_list, wall_pairs, fluid_state, ghosts, walls)
    peak = lax.pmax(peak[0, 0], ("orb", "wall"))
    time_step = courant * jnp.sqrt(smoothing / (peak + 1e-06))
    return (rates.reshape(-1), acceleration, time_step)


def solution(mesh):
    return jax.shard_map(
        per_device,
        mesh=mesh,
        in_specs=(
            P(None, ("orb", "wall")),
            P(None, ("orb", "wall")),
            P(("orb", "wall"), None),
            P(None, ("orb", "wall")),
            P(("orb", "wall")),
            P(("orb", "wall"), None),
        ),
        out_specs=(P(("orb", "wall")), P(None, ("orb", "wall")), P()),
        check_vma=False,
    )
```

time: 215 us -> 161 us (0.75)
  other arithmetic: 77.9 us -> 2.78 us
  Pallas kernels: 0 us -> 51.7 us
  local copies, waits for them, and re-layouts: 29.1 us -> 4.82 us
    pallas_call x0 -> x1, Pallas kernels: none -> 51.7 us  [pair_forces(): pl.pallas_call(pair_kernel, name='pair_forces', out_shape=(jax.ShapeDtype...]
    reduce_sum x61 -> x0, other arithmetic: 38.9 us -> none  [the longest x24 20 us: kernel_parts(): dist_sq = jnp.sum(offset * offset, axis=1)]
    mul x24 -> x0, other arithmetic: 31.9 us -> none  [the longest x12 27.9 us: block_terms(): weight = mass_row * (press_term * grad_scale + cohesion * pull)]
    gather x24 -> x0, local copies, waits for them, and re-layouts: 13.8 us -> none  [per_block(): return block_terms(target, candidates[pair_row], wall_cands[wall_row])]
    dynamic_slice x24 -> x0, local copies, waits for them, and re-layouts: 8.52 us -> none  [per_device(): lax.map(per_group, (grouped(own_blocks), grouped(pair_list), grouped(wall...]
    ppermute x14 -> x9, waiting for transfers between devices: 6.58 us -> 4.91 us  [the longest x7 4.91 us: per_device(): lax.ppermute(outgoing[q - 1], 'orb', [(i, i ^ q) for i in range(size)])]
    ppermute x14 -> x9, starting transfers between devices: 16.2 us -> 15.2 us  [the longest x7 9.87 us: per_device(): lax.ppermute(outgoing[q - 1], 'orb', [(i, i ^ q) for i in range(size)])]
  transfers between devices with their start and end apart: 14 -> 9, of which waited for: 2 -> 2; matrix products, arithmetic and copies ran while one was open for 2% -> 2% of each run, Pallas kernels for 0% -> 0%
where the time goes in v1:
time: 161 us
  blocking collectives  78.9 us (49%)
  Pallas kernels  51.7 us (32%)
  starting transfers between devices  15.2 us (9%)
  waiting for transfers between devices  4.91 us (3%)
  local copies, waits for them, and re-layouts  4.82 us (3%)
  other arithmetic  2.78 us (2%)
  between operations  2.6 us (2%)
    pmax x1, blocking collectives, per_device(): peak = lax.pmax(peak[0, 0], ('orb', 'wall'))  78.9 us
    pallas_call x1, Pallas kernels, pair_forces(): pl.pallas_call(pair_kernel, name='pair_forces', out_shape=(jax.ShapeDtype...  51.7 us
    ppermute x7, starting transfers between devices, per_device(): lax.ppermute(outgoing[q - 1], 'orb', [(i, i ^ q) for i in range(size)])  9.87 us
    ppermute x7, waiting for transfers between devices, per_device(): lax.ppermute(outgoing[q - 1], 'orb', [(i, i ^ q) for i in range(size)])  4.91 us
    ppermute x1, starting transfers between devices, padded(): low = lax.ppermute(block[:, block.shape[1] - width:], axis, forward)  4.01 us
  transfers between devices with their start and end apart: 9, of which 2 were waited for; matrix products, arithmetic and copies ran while one was open for 2% of the time, Pallas kernels for 0%

profile of v1, /device:TPU:1, one launch (start us, length us, event | category | flops | bytes accessed | tf_op | source)
XLA Modules:
  0.0 160.8 jit_solution(4400559995724139075)
XLA Ops:
  0.6 0.7 fusion
  1.4 0.7 bitcast_select_fusion
  2.1 0.7 pad_maximum_fusion.2
  2.8 4.0 %collective-permute-start.7 = (f32[4,128]{1,0:T(4,128)S(1)}, f32[4,128]{1,0:T(4,128)S(1)}, u32[]{:S(2)}, u32[]{:S(2)}) collective-permute-start(f32[4,128]{1,0:T(4,128)S(1)} %get-tuple-element.16), channel_id=1, source_target_pairs={{0,1},{1,2},{2,3},{4,5},{5,6},{6,7},{8,9},{9,10},{10,11},{12,13},{... | collective-permute-start | bytes 6152 | tf_op jit(solution)/shard_map/ppermute | solution.py:324
  6.8 1.3 collective-permute-start.8
  8.1 0.1 reshape.43
  8.2 1.5 gather_fusion
  9.7 0.0 copy-start.4
  9.7 1.0 collective-permute-start
  10.8 1.6 %collective-permute-start.1 = (f32[6,8,128]{2,1,0:T(8,128)S(1)}, f32[6,8,128]{2,1,0:T(8,128)S(1)}, u32[]{:S(2)}, u32[]{:S(2)}) collective-permute-start(f32[6,8,128]{2,1,0:T(8,128)S(1)} %get-tuple-element.14), channel_id=1, source_target_pairs={{0,8},{4,12},{8,0},{12,4},{16,24},{20,28},{24,16},{28,20},{32,40},... | collective-permute-start | bytes 73736 | tf_op jit(solution)/shard_map/ppermute | solution.py:334
  12.4 0.1 collective-permute-start.2
  12.5 0.7 copy.10.wpair_ref
  13.2 0.7 copy.9.pair_ref
  13.9 3.0 %collective-permute-start.3 = (f32[6,8,128]{2,1,0:T(8,128)S(1)}, f32[6,8,128]{2,1,0:T(8,128)S(1)}, u32[]{:S(2)}, u32[]{:S(2)}) collective-permute-start(f32[6,8,128]{2,1,0:T(8,128)S(1)} %get-tuple-element.12), channel_id=1, source_target_pairs={{0,16},{4,20},{8,24},{12,28},{16,0},{20,4},{24,8},{28,12},{32,48},... | collective-permute-start | bytes 73736 | tf_op jit(solution)/shard_map/ppermute | solution.py:334
  16.9 0.3 collective-permute-start.4
  17.2 0.6 pad_maximum_fusion.wall_ref
  17.8 3.7 %collective-permute-start.5 = (f32[6,8,128]{2,1,0:T(8,128)S(1)}, f32[6,8,128]{2,1,0:T(8,128)S(1)}, u32[]{:S(2)}, u32[]{:S(2)}) collective-permute-start(f32[6,8,128]{2,1,0:T(8,128)S(1)} %get-tuple-element.10), channel_id=1, source_target_pairs={{0,24},{4,28},{8,16},{12,20},{16,8},{20,12},{24,0},{28,4},{32,56},... | collective-permute-start | bytes 73736 | tf_op jit(solution)/shard_map/ppermute | solution.py:334
  21.5 0.1 collective-permute-start.6
  21.7 1.1 collective-permute-done.5
  22.8 3.8 %collective-permute-done.6 = f32[6,8,128]{2,1,0:T(8,128)S(1)} collective-permute-done((f32[6,8,128]{2,1,0:T(8,128)S(1)}, f32[6,8,128]{2,1,0:T(8,128)S(1)}, u32[]{:S(2)}, u32[]{:S(2)}) %collective-permute-start.6) | collective-permute-done | bytes 24608 | tf_op jit(solution)/shard_map/ppermute | solution.py:334
  26.6 0.7 copy-done
  27.2 51.7 %pair_forces.1 = (f32[24,128]{1,0:T(8,128)}, f32[3,3072]{1,0:T(4,128)}, f32[8,128]{1,0:T(8,128)}) custom-call(s32[24,14]{1,0:T(8,128)} %copy.9.pair_ref, s32[24,4]{1,0:T(8,128)} %copy.10.wpair_ref, f32[8,3072]{1,0:T(8,128)} %own_ref.1, f32[336,128]{1,0:T(8,128)} %bitcast.13, f32[4,1024]{1,0:T(4,128)} %pad_maximum_fusion.wall_ref), custom_call_target="tpu_custom_call" | custom-call | tf_op jit(solution)/shard_map/pair_forces/pallas_call | solution.py:290
  78.9 1.2 slice.47
  80.1 78.9 %pmax.7 = f32[]{:T(128)} all-reduce(f32[]{:T(128)} %bitcast.4), channel_id=1, replica_groups=mesh['orb'=64,'wall'=4] {'orb','wall'}, use_global_device_ids=true, to_apply=%region_0.0 | all-reduce | flops 1 | bytes 8 | tf_op jit(solution)/shard_map/pmax | solution.py:341
  (25 shorter events, 0.1 us)
Async XLA Ops:
  2.1 6.0 %copy-start.3 = (s32[7,6]{1,0:T(8,128)S(1)}, s32[7,6]{1,0:T(8,128)}, u32[]{:S(2)}) copy-start(s32[7,6]{1,0:T(8,128)} %param.7) | copy-start | bytes 508
  2.8 11.1 %collective-permute-start.7 = (f32[4,128]{1,0:T(4,128)S(1)}, f32[4,128]{1,0:T(4,128)S(1)}, u32[]{:S(2)}, u32[]{:S(2)}) collective-permute-start(f32[4,128]{1,0:T(4,128)S(1)} %get-tuple-element.16), channel_id=1, source_target_pairs={{0,1},{1,2},{2,3},{4,5},{5,6},{6,7},{8,9},{9,10},{10,11},{12,13},{... | collective-permute-start | bytes 6152 | tf_op jit(solution)/shard_map/ppermute | solution.py:324
  6.8 10.1 %collective-permute-start.8 = (f32[4,128]{1,0:T(4,128)S(1)}, f32[4,128]{1,0:T(4,128)S(1)}, u32[]{:S(2)}, u32[]{:S(2)}) collective-permute-start(f32[4,128]{1,0:T(4,128)S(1)} %get-tuple-element.17), channel_id=1, source_target_pairs={{1,0},{2,1},{3,2},{5,4},{6,5},{7,6},{9,8},{10,9},{11,10},{13,12},{... | collective-permute-start | bytes 6152 | tf_op jit(solution)/shard_map/ppermute | solution.py:325
  9.7 2.8 %copy-start.4 = (s32[24,4]{0,1:T(4,128)S(1)}, s32[24,4]{0,1:T(4,128)}, u32[]{:S(2)}) copy-start(s32[24,4]{0,1:T(4,128)} %param.11) | copy-start | bytes 1156
  9.7 8.0 %collective-permute-start = (f32[6,8,128]{2,1,0:T(8,128)S(1)}, f32[6,8,128]{2,1,0:T(8,128)S(1)}, u32[]{:S(2)}, u32[]{:S(2)}) collective-permute-start(f32[6,8,128]{2,1,0:T(8,128)S(1)} %get-tuple-element.15), channel_id=1, source_target_pairs={{0,4},{4,0},{8,12},{12,8},{16,20},{20,16},{24,28},{28,24},{32,36},... | collective-permute-start | bytes 73736 | tf_op jit(solution)/shard_map/ppermute | solution.py:334
  10.8 2.4 %copy-start.2 = (s32[24,14]{0,1:T(8,128)S(1)}, s32[24,14]{0,1:T(8,128)}, u32[]{:S(2)}) copy-start(s32[24,14]{0,1:T(8,128)} %param.8) | copy-start | bytes 4036
  10.8 10.7 %collective-permute-start.1 = (f32[6,8,128]{2,1,0:T(8,128)S(1)}, f32[6,8,128]{2,1,0:T(8,128)S(1)}, u32[]{:S(2)}, u32[]{:S(2)}) collective-permute-start(f32[6,8,128]{2,1,0:T(8,128)S(1)} %get-tuple-element.14), channel_id=1, source_target_pairs={{0,8},{4,12},{8,0},{12,4},{16,24},{20,28},{24,16},{28,20},{32,40},... | collective-permute-start | bytes 73736 | tf_op jit(solution)/shard_map/ppermute | solution.py:334
  12.4 9.2 %collective-permute-start.2 = (f32[6,8,128]{2,1,0:T(8,128)S(1)}, f32[6,8,128]{2,1,0:T(8,128)S(1)}, u32[]{:S(2)}, u32[]{:S(2)}) collective-permute-start(f32[6,8,128]{2,1,0:T(8,128)S(1)} %get-tuple-element.13), channel_id=1, source_target_pairs={{0,12},{4,8},{8,4},{12,0},{16,28},{20,24},{24,20},{28,16},{32,44},... | collective-permute-start | bytes 73736 | tf_op jit(solution)/shard_map/ppermute | solution.py:334
  13.2 3.9 %copy-start.1 = (f32[4,768]{1,0:T(4,128)S(1)}, f32[4,768]{1,0:T(4,128)}, u32[]{:S(2)}) copy-start(f32[4,768]{1,0:T(4,128)} %param.9) | copy-start | bytes 36868
  13.9 7.7 %collective-permute-start.3 = (f32[6,8,128]{2,1,0:T(8,128)S(1)}, f32[6,8,128]{2,1,0:T(8,128)S(1)}, u32[]{:S(2)}, u32[]{:S(2)}) collective-permute-start(f32[6,8,128]{2,1,0:T(8,128)S(1)} %get-tuple-element.12), channel_id=1, source_target_pairs={{0,16},{4,20},{8,24},{12,28},{16,0},{20,4},{24,8},{28,12},{32,48},... | collective-permute-start | bytes 73736 | tf_op jit(solution)/shard_map/ppermute | solution.py:334
  16.9 4.8 %collective-permute-start.4 = (f32[6,8,128]{2,1,0:T(8,128)S(1)}, f32[6,8,128]{2,1,0:T(8,128)S(1)}, u32[]{:S(2)}, u32[]{:S(2)}) collective-permute-start(f32[6,8,128]{2,1,0:T(8,128)S(1)} %get-tuple-element.11), channel_id=1, source_target_pairs={{0,20},{4,16},{8,28},{12,24},{16,4},{20,0},{24,12},{28,8},{32,52},... | collective-permute-start | bytes 73736 | tf_op jit(solution)/shard_map/ppermute | solution.py:334
  17.8 5.0 %collective-permute-start.5 = (f32[6,8,128]{2,1,0:T(8,128)S(1)}, f32[6,8,128]{2,1,0:T(8,128)S(1)}, u32[]{:S(2)}, u32[]{:S(2)}) collective-permute-start(f32[6,8,128]{2,1,0:T(8,128)S(1)} %get-tuple-element.10), channel_id=1, source_target_pairs={{0,24},{4,28},{8,16},{12,20},{16,8},{20,12},{24,0},{28,4},{32,56},... | collective-permute-start | bytes 73736 | tf_op jit(solution)/shard_map/ppermute | solution.py:334
  21.5 5.1 %collective-permute-start.6 = (f32[6,8,128]{2,1,0:T(8,128)S(1)}, f32[6,8,128]{2,1,0:T(8,128)S(1)}, u32[]{:S(2)}, u32[]{:S(2)}) collective-permute-start(f32[6,8,128]{2,1,0:T(8,128)S(1)} %get-tuple-element.9), channel_id=1, source_target_pairs={{0,28},{4,24},{8,20},{12,16},{16,12},{20,8},{24,4},{28,0},{32,60},... | collective-permute-start | bytes 73736 | tf_op jit(solution)/shard_map/ppermute | solution.py:334
  26.6 0.7 copy-start

commit v2 on v1

--- a/solution.py
+++ b/solution.py
@@ -29,7 +29,9 @@
 center = 0.3
 inv_support = 1.0 / support
 eps_scaled = 0.0001 / support**2
-visc_scaled = visc_coeff * -grad_coeff / support
+pull_scale = 4.0 * cohesion
+wall_pull_scale = 4.0 * adhesion
+visc_scaled = visc_coeff * -grad_coeff / support / pull_scale
 
 F32 = jnp.float32
 BF16 = jnp.bfloat16
@@ -142,6 +144,7 @@
 def pair_kernel(
     pair_ref, wpair_ref, own_ref, ghost_ref, wall_ref, rate_ref, accel_ref, peak_ref,
     cand, wcand, jf32, if32, wf32, cl32, wc32, jf, tf, wf, cl, wc, sums, wsums,
+    geo0, geo1, wgeo0, wgeo1,
 ):
     for b in range(NB):
         cand[8 * b : 8 * b + 8, :] = own_ref[:, LN * b : LN * b + LN]
@@ -218,39 +221,47 @@
 
     lax.fori_loop(0, NW, build_wall, 0)
 
-    def block(b, carry):
+    def geometry(b, geo, wgeo):
         weights = tf[b]
+        lhs = jnp.concatenate([jf[pair_ref[k, b]] for k in range(K)], axis=0)
+        geo[...] = jnp.dot(lhs, weights, preferred_element_type=F32)
+        lhs = jnp.concatenate([wf[wpair_ref[k, b]] for k in range(KW)], axis=0)
+        wgeo[...] = jnp.dot(lhs, weights[:, :LN], preferred_element_type=F32)
+
+    def summed(columns, cubed, pull):
+        sh, sl = two_terms(cubed)
+        uh, ul = two_terms(pull)
+        mat = jnp.concatenate(
+            [jnp.concatenate([sh, uh], axis=1), jnp.concatenate([sl, ul], axis=1)], axis=0
+        )
+        return jnp.dot(columns, mat, preferred_element_type=F32)
+
+    def forces(b, geo, wgeo):
         total = jnp.zeros((32, 2 * LN), F32)
         for k in range(K):
-            j = pair_ref[b, k]
-            geo = jnp.dot(jf[j], weights, preferred_element_type=F32)
-            s, cubed = falloff_of(geo[:, :LN])
-            root = lax.rsqrt(geo[:, 2 * LN :])
-            drag = jnp.minimum(geo[:, LN : 2 * LN], 0.0) * (root * root)
-            pull = cubed * (drag + (3.0 * cohesion - 4.0 * cohesion * s))
-            sh, sl = two_terms(cubed)
-            uh, ul = two_terms(pull)
-            mat = jnp.concatenate(
-                [jnp.concatenate([sh, uh], axis=1), jnp.concatenate([sl, ul], axis=1)], axis=0
-            )
-            total += jnp.dot(cl[j], mat, preferred_element_type=F32)
+            tile = pl.ds(k * LN, LN)
+            s, cubed = falloff_of(geo[tile, :LN])
+            root = lax.rsqrt(geo[tile, 2 * LN :])
+            drag = jnp.minimum(geo[tile, LN : 2 * LN], 0.0) * (root * root)
+            total += summed(cl[pair_ref[k, b]], cubed, cubed * (drag - s))
         sums[b] = total[:16] + total[16:]
-        wtotal = jnp.zeros((16, 2 * LN), F32)
+        total = jnp.zeros((16, 2 * LN), F32)
         for k in range(KW):
-            j = wpair_ref[b, k]
-            geo = jnp.dot(wf[j], weights[:, :LN], preferred_element_type=F32)
-            s, cubed = falloff_of(geo)
-            pull = cubed * (3.0 * adhesion - 4.0 * adhesion * s)
-            sh, sl = two_terms(cubed)
-            uh, ul = two_terms(pull)
-            mat = jnp.concatenate(
-                [jnp.concatenate([sh, uh], axis=1), jnp.concatenate([sl, ul], axis=1)], axis=0
-            )
-            wtotal += jnp.dot(wc[j], mat, preferred_element_type=F32)
-        wsums[b] = wtotal[:8] + wtotal[8:]
+            s, cubed = falloff_of(wgeo[pl.ds(k * LN, LN), :])
+            total += summed(wc[wpair_ref[k, b]], cubed, cubed * s)
+        wsums[b] = total[:8] + total[8:]
+
+    geometry(0, geo0, wgeo0)
+
+    def two_blocks(t, carry):
+        b = 2 * t
+        geometry(b + 1, geo1, wgeo1)
+        forces(b, geo0, wgeo0)
+        geometry(jnp.minimum(b + 2, NB - 1), geo0, wgeo0)
+        forces(b + 1, geo1, wgeo1)
         return carry
 
-    lax.fori_loop(0, NB, block, 0)
+    lax.fori_loop(0, NB // 2, two_blocks, 0)
 
     def take(ref, row, lane):
         return ref[:, row, lane : lane + LN]
@@ -273,7 +284,10 @@
             ty[c] * (spart[0] + 2.0 * wspart[0]) - (spart[1 + c] + 2.0 * wspart[1 + c])
         )
         pressed += ty[c] * spart[8] - spart[9 + c]
-        pulled = ty[c] * (upart[0] + wupart[0]) - (upart[1 + c] + wupart[1 + c])
+        near = ty[c] * spart[0] - spart[1 + c]
+        wnear = ty[c] * wspart[0] - wspart[1 + c]
+        pulled = 3.0 * cohesion * near + pull_scale * (ty[c] * upart[0] - upart[1 + c])
+        pulled += 3.0 * adhesion * wnear - wall_pull_scale * (ty[c] * wupart[0] - wupart[1 + c])
         force = (-grad_coeff * support) * pressed - support * pulled
         if c == 2:
             force = force - gravity
@@ -312,35 +326,183 @@
             pltpu.VMEM((NW, 16, 2 * LN), BF16),
             pltpu.VMEM((NB, 16, 2 * LN), F32),
             pltpu.VMEM((NB, 8, 2 * LN), F32),
+            pltpu.VMEM((K * LN, 3 * LN), F32),
+            pltpu.VMEM((K * LN, 3 * LN), F32),
+            pltpu.VMEM((KW * LN, LN), F32),
+            pltpu.VMEM((KW * LN, LN), F32),
         ],
         **kw,
     )(pairs, wpairs, own, ghosts, walls)
 
 
-def padded(block, axis, width):
-    count = lax.axis_size(axis)
-    forward = [(i, i + 1) for i in range(count - 1)]
-    backward = [(target, source) for source, target in forward]
-    low = lax.ppermute(block[:, block.shape[1] - width :], axis, forward)
-    high = lax.ppermute(block[:, :width], axis, backward)
-    return jnp.concatenate([low, block, high], axis=1)
+MESH = pl.DeviceIdType.MESH
+
+
+def flipped(place, pattern):
+    partner = place
+    for bit in (1, 2, 4):
+        if pattern & bit:
+            partner = partner + bit - 2 * bit * lax.rem(lax.div(place, bit), 2)
+    return partner
+
+
+def exchange_kernel(
+    ghost_ref, count_ref, own_ref, wall_ref, ghosts_ref, walls_ref,
+    blocks, outgoing, edges, edges_in, send_sems, recv_sems,
+):
+    orb = lax.axis_index("orb")
+    place = lax.axis_index("wall")
+    places = lax.axis_size("wall")
+    partners = [flipped(orb, q) for q in range(1, 8)]
+    above, below = lax.rem(place + 1, places), lax.rem(place + places - 1, places)
+
+    barrier = pltpu.get_barrier_semaphore()
+    for partner in partners:
+        pl.semaphore_signal(barrier, inc=1, device_id={"orb": partner}, device_id_type=MESH)
+    for partner in (above, below):
+        pl.semaphore_signal(barrier, inc=1, device_id={"wall": partner}, device_id_type=MESH)
+
+    lane = lax.broadcasted_iota(jnp.int32, (1, LN), 1)
+    for b in range(WB):
+        block = wall_ref[:, LN * b : LN * b + LN]
+        live = jnp.where(lane < count_ref[b], block[3:4], 0.0)
+        block = jnp.concatenate([block[:3], live], axis=0)
+        walls_ref[:, LN * (b + 1) : LN * (b + 2)] = block
+        if b == 0:
+            edges[0] = block
+        if b == WB - 1:
+            edges[1] = block
+    for b in range(NB):
+        blocks[b] = own_ref[:, LN * b : LN * b + LN]
+    for q in range(7):
+        for g in range(GH):
+            outgoing[q, 8 * g : 8 * g + 8, :] = blocks[ghost_ref[q, g]]
+
+    pl.semaphore_wait(barrier, 9)
+    copies = []
+    for slot, partner in enumerate((below, above)):
+        copies.append(
+            pltpu.make_async_remote_copy(
+                src_ref=edges.at[slot],
+                dst_ref=edges_in.at[slot],
+                send_sem=send_sems.at[7 + slot],
+                recv_sem=recv_sems.at[7 + slot],
+                device_id={"wall": partner},
+                device_id_type=MESH,
+            )
+        )
+    rows = 8 * GH
+    for q in (6, 5, 3, 4, 2, 1, 0):
+        copies.append(
+            pltpu.make_async_remote_copy(
+                src_ref=outgoing.at[q],
+                dst_ref=ghosts_ref.at[pl.ds(q * rows, rows)],
+                send_sem=send_sems.at[q],
+                recv_sem=recv_sems.at[q],
+                device_id={"orb": partners[q]},
+                device_id_type=MESH,
+            )
+        )
+    for copy in copies:
+        copy.start()
+    for copy in copies[:2]:
+        copy.wait()
+    walls_ref[:, :LN] = jnp.where(place > 0, edges_in[1], 0.0)
+    walls_ref[:, LN * (NW - 1) :] = jnp.where(place < places - 1, edges_in[0], 0.0)
+    for copy in copies[2:]:
+        copy.wait()
+
+
+def exchange(ghost_list, wall_count, own, walls):
+    vmem = pl.BlockSpec(memory_space=pltpu.VMEM)
+    smem = pl.BlockSpec(memory_space=pltpu.SMEM)
+    return pl.pallas_call(
+        exchange_kernel,
+        name="exchange",
+        out_shape=(
+            jax.ShapeDtypeStruct((7 * GH * 8, LN), F32),
+            jax.ShapeDtypeStruct((4, NW * LN), F32),
+        ),
+        in_specs=[smem, smem, vmem, vmem],
+        out_specs=(vmem, vmem),
+        scratch_shapes=[
+            pltpu.VMEM((NB, 8, LN), F32),
+            pltpu.VMEM((7, GH * 8, LN), F32),
+            pltpu.VMEM((2, 4, LN), F32),
+            pltpu.VMEM((2, 4, LN), F32),
+            pltpu.SemaphoreType.DMA((9,)),
+            pltpu.SemaphoreType.DMA((9,)),
+        ],
+        compiler_params=pltpu.CompilerParams(collective_id=0, has_side_effects=True),
+    )(ghost_list, wall_count, own, walls)
+
+
+def rounds():
+    orb = lax.axis_index("orb")
+    place = lax.axis_index("wall")
+    x, rest = lax.div(orb, 16), lax.rem(orb, 16)
+    mine = x * 4 + place
+    first = []
+    for t in range(1, 16):
+        other = lax.rem(mine + t, 16)
+        first.append({"orb": lax.div(other, 4) * 16 + rest, "wall": lax.rem(other, 4)})
+    second = [{"orb": x * 16 + lax.rem(rest + t, 16), "wall": place} for t in range(1, 16)]
+    return first, second
+
+
+def peak_kernel(peak_ref, step_ref, held, slots, send_sems, recv_sems):
+    phases = rounds()
+    barrier = pltpu.get_barrier_semaphore()
+    for phase in phases:
+        for partner in phase:
+            pl.semaphore_signal(barrier, inc=1, device_id=partner, device_id_type=MESH)
+    held[0] = peak_ref[0:1, :]
+    pl.semaphore_wait(barrier, 30)
+    for n, phase in enumerate(phases):
+        copies = [
+            pltpu.make_async_remote_copy(
+                src_ref=held.at[n],
+                dst_ref=slots.at[n, t],
+                send_sem=send_sems.at[n, t],
+                recv_sem=recv_sems.at[n, t],
+                device_id=partner,
+                device_id_type=MESH,
+            )
+            for t, partner in enumerate(phase)
+        ]
+        for copy in copies:
+            copy.start()
+        best = held[n]
+        for t, copy in enumerate(copies):
+            copy.wait()
+            best = jnp.maximum(best, slots[n, t])
+        held[n + 1] = best
+    step = courant * jnp.sqrt(smoothing / (best + 1e-06))
+    step_ref[0, 0] = jnp.max(step)
+
+
+def global_step(peak):
+    return pl.pallas_call(
+        peak_kernel,
+        name="global_step",
+        out_shape=jax.ShapeDtypeStruct((1, 1), F32),
+        in_specs=[pl.BlockSpec(memory_space=pltpu.VMEM)],
+        out_specs=pl.BlockSpec(memory_space=pltpu.SMEM),
+        scratch_shapes=[
+            pltpu.VMEM((3, 1, LN), F32),
+            pltpu.VMEM((2, 15, 1, LN), F32),
+            pltpu.SemaphoreType.DMA((2, 15)),
+            pltpu.SemaphoreType.DMA((2, 15)),
+        ],
+        compiler_params=pltpu.CompilerParams(collective_id=1, has_side_effects=True),
+    )(peak)
 
 
 def per_device(fluid_state, ghost_list, pair_list, wall_state, wall_count, wall_pairs):
-    own_blocks = jnp.transpose(fluid_state.reshape(8, NB, LN), (1, 0, 2))
-    outgoing = own_blocks[ghost_list]
-    size = lax.axis_size("orb")
-    arrived = [
-        lax.ppermute(outgoing[q - 1], "orb", [(i, i ^ q) for i in range(size)]) for q in range(1, 8)
-    ]
-    ghosts = jnp.concatenate(arrived).reshape(-1, LN)
-    alive = (jnp.arange(LN, dtype=jnp.int32)[None, :] < wall_count[:, None]).astype(F32).reshape(-1)
-    wall_live = jnp.concatenate([wall_state[0:3], wall_state[3:4] * alive[None, :]], axis=0)
-    walls = padded(wall_live, "wall", EB * LN)
-    rates, acceleration, peak = pair_forces(pair_list, wall_pairs, fluid_state, ghosts, walls)
-    peak = lax.pmax(peak[0, 0], ("orb", "wall"))
-    time_step = courant * jnp.sqrt(smoothing / (peak + 1e-06))
-    return (rates.reshape(-1), acceleration, time_step)
+    ghosts, walls = exchange(ghost_list, wall_count, fluid_state, wall_state)
+    rates, acceleration, peak = pair_forces(pair_list.T, wall_pairs.T, fluid_state, ghosts, walls)
+    step = global_step(peak)
+    return (rates.reshape(-1), acceleration, step.reshape(()))
 
 
 def solution(mesh):

time: 161 us -> 63.7 us (0.40)
  blocking collectives: 78.9 us -> 0 us
  starting transfers between devices: 15.2 us -> 0 us
  Pallas kernels: 51.7 us -> 61 us
  waiting for transfers between devices: 4.91 us -> 0 us
  local copies, waits for them, and re-layouts: 4.82 us -> 0 us
  other arithmetic: 2.78 us -> 0 us
    pmax x1 -> x0, blocking collectives: 78.9 us -> none  [per_device(): peak = lax.pmax(peak[0, 0], ('orb', 'wall'))]
    pallas_call x0 -> x2, Pallas kernels: none -> 30.5 us  [the longest x1 16.7 us: global_step(): pl.pallas_call(peak_kernel, name='global_step', out_shape=jax.ShapeDtypeS...]
    pallas_call x1, Pallas kernels: 51.7 us -> 30.6 us  [pair_forces(): pl.pallas_call(pair_kernel, name='pair_forces', out_shape=(jax.ShapeDtype...]
    ppermute x9 -> x0, starting transfers between devices: 15.2 us -> none  [the longest x7 9.87 us: per_device(): lax.ppermute(outgoing[q - 1], 'orb', [(i, i ^ q) for i in range(size)])]
    ppermute x9 -> x0, waiting for transfers between devices: 4.91 us -> none  [the longest x7 4.91 us: per_device(): lax.ppermute(outgoing[q - 1], 'orb', [(i, i ^ q) for i in range(size)])]
    unnamed x18 -> x0, local copies, waits for them, and re-layouts: 2.06 us -> none
  transfers between devices with their start and end apart: 9 -> 0, of which waited for: 2 -> 0; matrix products, arithmetic and copies ran while one was open for 2% -> 0% of each run, Pallas kernels for 0% -> 0%
where the time goes in v2:
time: 63.7 us; the launch traced here: 63.4 us
  Pallas kernels  61 us (96%)
  between operations  2.4 us (4%)
    pallas_call x1, Pallas kernels, pair_forces(): pl.pallas_call(pair_kernel, name='pair_forces', out_shape=(jax.ShapeDtype...  30.6 us
    pallas_call x1, Pallas kernels, global_step(): pl.pallas_call(peak_kernel, name='global_step', out_shape=jax.ShapeDtypeS...  16.7 us
    pallas_call x1, Pallas kernels, exchange(): pl.pallas_call(exchange_kernel, name='exchange', out_shape=(jax.ShapeDtyp...  13.7 us

profile of v2, /device:TPU:1, one launch (start us, length us, event | category | flops | bytes accessed | tf_op | source)
XLA Modules:
  0.0 63.4 jit_solution(15872694517690166850)
XLA Ops:
  0.6 13.7 %exchange.1 = (f32[336,128]{1,0:T(8,128)}, f32[4,1024]{1,0:T(4,128)}) custom-call(s32[7,6]{1,0:T(8,128)} %ghost_ref.1, s32[6]{0:T(128)} %count_ref.1, f32[8,3072]{1,0:T(8,128)} %own_ref.3, f32[4,768]{1,0:T(4,128)} %wall_ref.1), custom_call_target="tpu_custom_call" | custom-call | tf_op jit(solution)/shard_map/exchange/pallas_call | solution.py:419
  14.4 30.6 %pair_forces.1 = (f32[24,128]{1,0:T(8,128)}, f32[3,3072]{1,0:T(4,128)}, f32[8,128]{1,0:T(8,128)}) custom-call(s32[14,24]{1,0:T(8,128)} %bitcast.4, s32[4,24]{1,0:T(4,128)} %bitcast.5, f32[8,3072]{1,0:T(8,128)} %own_ref.3, f32[336,128]{1,0:T(8,128)} %get-tuple-element.8.ghost_ref, f32[4,1024]{1,0:T(4,128)} %get-tuple-element.9.wall_ref), custom_call_target="tpu_custom_call" | custom-call | tf_op jit(solution)/shard_map/pair_forces/pallas_call | solution.py:304
  45.0 16.7 %global_step.1 = f32[1,1]{1,0:T(1,128)} custom-call(f32[8,128]{1,0:T(8,128)} %get-tuple-element.12.peak_ref), custom_call_target="tpu_custom_call" | custom-call | tf_op jit(solution)/shard_map/global_step/pallas_call | solution.py:485

commit v3 on v0

v3 whole, which is shorter than its diff:
```python
import jax
import jax.numpy as jnp
from jax import lax
from jax.experimental import pallas as pl
from jax.experimental.pallas import tpu as pltpu
from jax.sharding import PartitionSpec as P

NB = 24
K = 14
KW = 4
GH = 6
WB = 6
EB = 1
NC = NB + 7 * GH
NW = WB + 2 * EB
LN = 128

smoothing = 0.1
support = 0.3
kernel_norm = 21.0 / (2.0 * 3.141592653589793 * support**3)
grad_coeff = -20.0 / support**2 * kernel_norm
tait_coeff = 25.0 / 7.0
visc_coeff = 0.05
cohesion = 2000.0
adhesion = 2000.0
gravity = 9.81
courant = 0.25

center = 0.3
inv_support = 1.0 / support
eps_scaled = 0.0001 / support**2
pull_scale = 4.0 * cohesion
wall_pull_scale = 4.0 * adhesion
visc_scaled = visc_coeff * -grad_coeff / support / pull_scale
half_scale = 0.5 / visc_scaled

F32 = jnp.float32
BF16 = jnp.bfloat16


def split(value):
    parts = []
    for _ in range(2):
        high = value.astype(BF16).astype(F32)
        parts.append(high)
        value = value - high
    parts.append(value.astype(BF16).astype(F32))
    return parts


def two_terms(value):
    high = value.astype(BF16)
    return high, (value - high.astype(F32)).astype(BF16)


def pressure_of(density):
    return tait_coeff * (density**7 - 1.0)


def dot3(a, b):
    return a[0] * b[0] + a[1] * b[1] + a[2] * b[2]


def rows_of(block):
    return [block[c : c + 1] for c in range(block.shape[0])]


def stack(rows):
    return jnp.concatenate(rows, axis=0)


CROSS = ((0, 0), (0, 1), (0, 2), (1, 0), (1, 1), (2, 0))


def scaled_rows(block):
    rows = rows_of(block)
    y = [(row - center) * inv_support for row in rows[:3]]
    return y, rows[3:6], rows[6], rows[7]


def wide(groups):
    rows = stack(groups)
    spare = LN - rows.shape[0]
    return stack([rows, jnp.zeros((spare, LN), F32)]) if spare else rows


def source_tiles(block):
    y, v, rho, mass = scaled_rows(block)
    half = half_scale * rho
    one, zero = jnp.ones_like(mass), jnp.zeros_like(mass)
    norm, flow = dot3(y, y), dot3(v, y)
    terms = split(stack(y + v + [half, zero]))
    sums = split(stack([norm, flow, one, one, one, zero, zero, zero]))
    mixed = split(stack([half * c for c in y] + [half * norm, norm, one, one, one]))
    base = [terms[j] for j, _ in CROSS]
    push = pressure_of(rho) / (rho * rho)
    heavy = stack(y + v + [flow, one]) * mass
    pushed = heavy * push
    hh, hl = two_terms(heavy)
    ph, pl_ = two_terms(pushed)
    return wide(base + sums), wide(base + [mixed[j] for j, _ in CROSS]), stack([hh, ph, hl, pl_])


def wall_tiles(block):
    rows = rows_of(block)
    y = [(row - center) * inv_support for row in rows[:3]]
    mass = rows[3]
    one, zero = jnp.ones_like(mass), jnp.zeros_like(mass)
    terms = split(stack(y + [zero] * 5))
    sums = split(stack([dot3(y, y), zero, one, one, one, zero, zero, zero]))
    heavy = stack(y + [one, zero, zero, zero, zero]) * mass
    hh, hl = two_terms(heavy)
    return wide([terms[j] for j, _ in CROSS] + sums), stack([hh, hl])


def target_tiles(block):
    y, v, rho, mass = scaled_rows(block)
    half = half_scale * rho
    one, zero = jnp.ones_like(mass), jnp.zeros_like(mass)
    norm, flow = dot3(y, y), dot3(v, y)
    reach = norm + eps_scaled
    twice = [-2.0 * c for c in y]
    far = split(stack(twice + [zero] * 5))
    near = split(stack([-c for c in v] + [-c for c in y] + [zero] * 2))
    damp = split(stack([half * c for c in twice] + [zero] * 3 + [reach, zero]))
    mixed = split(stack(twice + [zero, half] + [zero] * 3))
    norms, flows, grounds = split(norm), split(flow), split(half * reach)
    mixed[0] = mixed[0] + stack([zero] * 3 + [one, zero] + grounds)
    far_sum = stack([one, zero] + norms + [zero] * 3)
    near_sum = stack([zero, one] + flows + [zero] * 3)
    return (
        wide([far[i] for _, i in CROSS] + [far_sum] * 3),
        wide([near[i] for _, i in CROSS] + [near_sum] * 3),
        wide([damp[i] for _, i in CROSS] + [mixed[i] for _, i in CROSS]),
    )


def falloff_of(dist_sq):
    dist_sq = jnp.maximum(dist_sq, 1e-30)
    s = jnp.maximum(1.0 - dist_sq * lax.rsqrt(dist_sq), 0.0)
    return s, s * s * s


def product(left, right):
    return jnp.dot(left, right, preferred_element_type=F32)


MESH = pl.DeviceIdType.MESH


def flipped(place, pattern):
    partner = place
    for bit in (1, 2, 4):
        if pattern & bit:
            partner = partner + bit - 2 * bit * lax.rem(lax.div(place, bit), 2)
    return partner


def rounds():
    orb = lax.axis_index("orb")
    place = lax.axis_index("wall")
    x, rest = lax.div(orb, 16), lax.rem(orb, 16)
    mine = x * 4 + place
    first = []
    for t in range(1, 16):
        other = lax.rem(mine + t, 16)
        first.append({"orb": lax.div(other, 4) * 16 + rest, "wall": lax.rem(other, 4)})
    second = [{"orb": x * 16 + lax.rem(rest + t, 16), "wall": place} for t in range(1, 16)]
    return first, second


def send(source, target, send_sem, recv_sem, device):
    return pltpu.make_async_remote_copy(
        src_ref=source,
        dst_ref=target,
        send_sem=send_sem,
        recv_sem=recv_sem,
        device_id=device,
        device_id_type=MESH,
    )


def step_kernel(
    pair_ref, wpair_ref, ghost_ref, count_ref, own_ref, wall_ref, rate_ref, accel_ref, step_ref,
    blocks, outgoing, arrived, edges, edges_in, held, slots,
    sf, se, sc, wf, wc, tf, te, tw, sums, wsums,
    near0, near1, damp0, damp1, wall0, wall1, own_rows,
    send_sems, recv_sems, peak_send, peak_recv,
):
    orb = lax.axis_index("orb")
    place = lax.axis_index("wall")
    places = lax.axis_size("wall")
    partners = [{"orb": flipped(orb, q)} for q in range(1, 8)]
    above = {"wall": lax.rem(place + 1, places)}
    below = {"wall": lax.rem(place + places - 1, places)}
    phases = rounds()

    barrier = pltpu.get_barrier_semaphore()
    greeted = [*partners, above, below, *phases[0], *phases[1]]
    for device in greeted:
        pl.semaphore_signal(barrier, inc=1, device_id=device, device_id_type=MESH)

    for b in range(NB):
        blocks[b] = own_ref[:, LN * b : LN * b + LN]
    for q in range(7):
        for g in range(GH):
            outgoing[q, 8 * g : 8 * g + 8, :] = blocks[ghost_ref[q, g]]
    lane_row = lax.broadcasted_iota(jnp.int32, (1, LN), 1)

    def live_block(b):
        block = wall_ref[:, LN * b : LN * b + LN]
        return stack([block[:3], jnp.where(lane_row < count_ref[b], block[3:4], 0.0)])

    edges[0] = live_block(0)
    edges[1] = live_block(WB - 1)

    row = lax.broadcasted_iota(jnp.int32, (LN, 2 * LN), 0)
    lane = lax.broadcasted_iota(jnp.int32, (LN, 2 * LN), 1)
    doubled = jnp.where(row == lane // 32 * 16 + lane % 16, 1.0, 0.0).astype(BF16)

    def keep_source(j, block):
        geometry, damping, columns = source_tiles(block)
        sf[j] = geometry.astype(BF16).T
        se[j] = damping.astype(BF16).T
        sc[j] = product(columns, doubled).astype(BF16)

    def build_own(b, carry):
        keep_source(b, blocks[b])
        return carry

    def keep_wall(b, block):
        geometry, columns = wall_tiles(block)
        wf[b] = geometry.astype(BF16).T
        wc[b] = product(columns, doubled).astype(BF16)

    def build_target(b, carry):
        distance, approach, damping = [t.astype(BF16) for t in target_tiles(blocks[b])]
        zero = jnp.zeros((LN, LN), BF16)
        tf[b] = jnp.concatenate([distance, approach], axis=1)
        for ref, tile in ((te, damping), (tw, distance)):
            ref[b, :LN, :LN] = tile
            ref[b, :LN, LN:] = zero
            ref[b, LN:, :LN] = zero
            ref[b, LN:, LN:] = tile
        return carry

    lax.fori_loop(0, NB, build_target, 0, unroll=2)
    for b in range(WB):
        keep_wall(b + 1, live_block(b))

    pl.semaphore_wait(barrier, len(greeted))
    edge_copies = [
        send(edges.at[n], edges_in.at[n], send_sems.at[7 + n], recv_sems.at[7 + n], device)
        for n, device in enumerate((below, above))
    ]
    ghost_copies = [
        send(outgoing.at[q], arrived.at[q], send_sems.at[q], recv_sems.at[q], partners[q])
        for q in range(7)
    ]
    for copy in edge_copies:
        copy.start()
    for q in (6, 5, 3, 4, 2, 1, 0):
        ghost_copies[q].start()

    lax.fori_loop(0, NB, build_own, 0, unroll=3)
    for copy in edge_copies:
        copy.wait()
    keep_wall(0, jnp.where(place > 0, edges_in[1], 0.0))
    keep_wall(NW - 1, jnp.where(place < places - 1, edges_in[0], 0.0))

    def gathered(ref, indices):
        return stack([ref[j] for j in indices])

    def paired(ref, indices):
        return jnp.concatenate([gathered(ref, indices[0::2]), gathered(ref, indices[1::2])], axis=1)

    def matrix(cubed, pull):
        terms = two_terms(cubed), two_terms(pull)
        rows = []
        for top in range(0, LN, 16):
            for part in range(2):
                rows.append(jnp.concatenate([t[part][top : top + 16] for t in terms], axis=1))
        return stack(rows)

    group = 4
    tall = KW // 2 * LN

    def wall_geometry(t, wall):
        for n in range(group):
            b = t * group + n
            tiles = paired(wf, [wpair_ref[k, b] for k in range(KW)])
            wall[n * tall : (n + 1) * tall] = product(tiles, tw[b])

    def wall_forces(t, wall):
        for n in range(group):
            b = t * group + n
            total = jnp.zeros((16, 2 * LN), F32)
            for k in range(KW):
                half, side = pl.ds(n * tall + k // 2 * LN, LN), k % 2 * LN
                s, cubed = falloff_of(wall[half, side : side + LN])
                total += product(wc[wpair_ref[k, b]], matrix(cubed, cubed * s))
            wsums[b] = total[:8] + total[8:]

    wall_geometry(0, wall0)

    def two_walls(t, carry):
        wall_geometry(2 * t + 1, wall1)
        wall_forces(2 * t, wall0)
        wall_geometry(jnp.minimum(2 * t + 2, NB // group - 1), wall0)
        wall_forces(2 * t + 1, wall1)
        return carry

    lax.fori_loop(0, NB // group // 2, two_walls, 0)

    for q in (0, 1, 2, 4, 3, 5, 6):
        ghost_copies[q].wait()

        def build_ghost(g, carry, q=q):
            keep_source(NB + q * GH + g, arrived[q, pl.ds(pl.multiple_of(g * 8, 8), 8), :])
            return carry

        lax.fori_loop(0, GH, build_ghost, 0, unroll=3)

    def geometry(b, near, damp):
        indices = [pair_ref[k, b] for k in range(K)]
        near[...] = product(gathered(sf, indices), tf[b])
        damp[...] = product(paired(se, indices), te[b])

    def forces(b, near, damp):
        total = jnp.zeros((32, 2 * LN), F32)
        for k in range(K):
            tile, half, side = pl.ds(k * LN, LN), pl.ds(k // 2 * LN, LN), k % 2 * LN
            s, cubed = falloff_of(near[tile, :LN])
            root = lax.rsqrt(damp[half, side : side + LN])
            drag = jnp.minimum(near[tile, LN:], 0.0) * (root * root)
            total += product(sc[pair_ref[k, b]], matrix(cubed, cubed * (drag - s)))
        sums[b] = total[:16] + total[16:]

    geometry(0, near0, damp0)

    def two_blocks(t, carry):
        b = 2 * t
        geometry(b + 1, near1, damp1)
        forces(b, near0, damp0)
        geometry(jnp.minimum(b + 2, NB - 1), near0, damp0)
        forces(b + 1, near1, damp1)
        return carry

    lax.fori_loop(0, NB // 2, two_blocks, 0)

    for b in range(NB):
        own_rows[8 * b : 8 * b + 8, :] = blocks[b]
    state = [own_rows[pl.ds(r, NB, stride=8), :] for r in range(8)]
    y = [(r - center) * inv_support for r in state[:3]]
    v, rho = state[3:6], state[6]
    push = pressure_of(rho) / (rho * rho)
    weigh = [sums[:, r, :LN] for r in range(16)]
    pull = [sums[:, r, LN:] for r in range(16)]
    wweigh = [wsums[:, r, :LN] for r in range(4)]
    wpull = [wsums[:, r, LN:] for r in range(4)]
    square = jnp.zeros((NB, LN), F32)
    forces_out = []
    for c in range(3):
        near = y[c] * weigh[7] - weigh[c]
        wnear = y[c] * wweigh[3] - wweigh[c]
        pressed = push * (near + 2.0 * wnear) + y[c] * weigh[15] - weigh[8 + c]
        pulled = 3.0 * cohesion * near + pull_scale * (y[c] * pull[7] - pull[c])
        pulled += 3.0 * adhesion * wnear - wall_pull_scale * (y[c] * wpull[3] - wpull[c])
        force = (-grad_coeff * support) * pressed - support * pulled
        if c == 2:
            force = force - gravity
        square += force * force
        forces_out.append(force)
    best = jnp.max(jnp.max(square, axis=0, keepdims=True), axis=1, keepdims=True)
    held[0] = jnp.broadcast_to(jnp.sqrt(best), (1, LN))

    def phase_copies(n):
        return [
            send(held.at[n], slots.at[n, t], peak_send.at[n, t], peak_recv.at[n, t], device)
            for t, device in enumerate(phases[n])
        ]

    copies = phase_copies(0)
    for copy in copies:
        copy.start()
    rate = (
        dot3(v, y) * (weigh[7] + wweigh[3])
        - dot3(v, [weigh[c] + wweigh[c] for c in range(3)])
        - dot3(weigh[3:6], y)
        + weigh[6]
    )
    rate_ref[...] = (grad_coeff * support) * rate
    for c in range(3):
        for b in range(NB):
            accel_ref[c : c + 1, LN * b : LN * b + LN] = forces_out[c][b : b + 1]
    for n in range(2):
        best = held[n]
        for t, copy in enumerate(copies):
            copy.wait()
            best = jnp.maximum(best, slots[n, t])
        held[n + 1] = best
        if n == 0:
            copies = phase_copies(1)
            for copy in copies:
                copy.start()
    step_ref[0, 0] = jnp.max(courant * jnp.sqrt(smoothing / (best + 1e-06)))


def per_device(fluid_state, ghost_list, pair_list, wall_state, wall_count, wall_pairs):
    vmem = pl.BlockSpec(memory_space=pltpu.VMEM)
    smem = pl.BlockSpec(memory_space=pltpu.SMEM)
    rates, acceleration, step = pl.pallas_call(
        step_kernel,
        name="step",
        out_shape=(
            jax.ShapeDtypeStruct((NB, LN), F32),
            jax.ShapeDtypeStruct((3, NB * LN), F32),
            jax.ShapeDtypeStruct((1, 1), F32),
        ),
        in_specs=[smem, smem, smem, smem, vmem, vmem],
        out_specs=(vmem, vmem, smem),
        scratch_shapes=[
            pltpu.VMEM((NB, 8, LN), F32),
            pltpu.VMEM((7, GH * 8, LN), F32),
            pltpu.VMEM((7, GH * 8, LN), F32),
            pltpu.VMEM((2, 4, LN), F32),
            pltpu.VMEM((2, 4, LN), F32),
            pltpu.VMEM((3, 1, LN), F32),
            pltpu.VMEM((2, 15, 1, LN), F32),
            pltpu.VMEM((NC, LN, LN), BF16),
            pltpu.VMEM((NC, LN, LN), BF16),
            pltpu.VMEM((NC, 32, 2 * LN), BF16),
            pltpu.VMEM((NW, LN, LN), BF16),
            pltpu.VMEM((NW, 16, 2 * LN), BF16),
            pltpu.VMEM((NB, LN, 2 * LN), BF16),
            pltpu.VMEM((NB, 2 * LN, 2 * LN), BF16),
            pltpu.VMEM((NB, 2 * LN, 2 * LN), BF16),
            pltpu.VMEM((NB, 16, 2 * LN), F32),
            pltpu.VMEM((NB, 8, 2 * LN), F32),
        ]
        + [pltpu.VMEM((K * LN, 2 * LN), F32)] * 2
        + [pltpu.VMEM((K // 2 * LN, 2 * LN), F32)] * 2
        + [pltpu.VMEM((4 * KW // 2 * LN, 2 * LN), F32)] * 2
        + [
            pltpu.VMEM((NB * 8, LN), F32),
            pltpu.SemaphoreType.DMA((9,)),
            pltpu.SemaphoreType.DMA((9,)),
            pltpu.SemaphoreType.DMA((2, 15)),
            pltpu.SemaphoreType.DMA((2, 15)),
        ],
        compiler_params=pltpu.CompilerParams(collective_id=0, has_side_effects=True),
    )(pair_list.T, wall_pairs.T, ghost_list, wall_count, fluid_state, wall_state)
    return (rates.reshape(-1), acceleration, step.reshape(()))


def solution(mesh):
    return jax.shard_map(
        per_device,
        mesh=mesh,
        in_specs=(
            P(None, ("orb", "wall")),
            P(None, ("orb", "wall")),
            P(("orb", "wall"), None),
            P(None, ("orb", "wall")),
            P(("orb", "wall")),
            P(("orb", "wall"), None),
        ),
        out_specs=(P(("orb", "wall")), P(None, ("orb", "wall")), P()),
        check_vma=False,
    )
```

time: 215 us -> 58.5 us (0.27)
  blocking collectives: 79.5 us -> 0 us
  other arithmetic: 77.9 us -> 0 us
  Pallas kernels: 0 us -> 53.1 us
  local copies, waits for them, and re-layouts: 29.1 us -> 2.73 us
  starting transfers between devices: 16.2 us -> 0 us
  waiting for transfers between devices: 6.58 us -> 0 us
    pmax x1 -> x0, blocking collectives: 79.5 us -> none  [per_device(): peak = lax.pmax(local_peak, ('orb', 'wall'))]
    pallas_call x0 -> x1, Pallas kernels: none -> 53.1 us  [per_device(): pl.pallas_call(step_kernel, name='step', out_shape=(jax.ShapeDtypeStruct(...]
    reduce_sum x61 -> x0, other arithmetic: 38.9 us -> none  [the longest x24 20 us: kernel_parts(): dist_sq = jnp.sum(offset * offset, axis=1)]
    mul x25 -> x0, other arithmetic: 32.6 us -> none  [the longest x12 27.9 us: block_terms(): weight = mass_row * (press_term * grad_scale + cohesion * pull)]
    ppermute x14 -> x0, starting transfers between devices: 16.2 us -> none  [the longest x12 10.9 us: swapped(): lax.ppermute(shard, axis, [(i, i ^ 1 << bit) for i in range(lax.axis_size...]
    gather x25 -> x0, local copies, waits for them, and re-layouts: 15.3 us -> none  [the longest x24 13.8 us: per_block(): return block_terms(target, candidates[pair_row], wall_cands[wall_row])]
    dynamic_slice x24 -> x0, local copies, waits for them, and re-layouts: 8.52 us -> none  [per_device(): lax.map(per_group, (grouped(own_blocks), grouped(pair_list), grouped(wall...]
    ppermute x14 -> x0, waiting for transfers between devices: 6.58 us -> none  [the longest x12 6.57 us: swapped(): lax.ppermute(shard, axis, [(i, i ^ 1 << bit) for i in range(lax.axis_size...]
  transfers between devices with their start and end apart: 14 -> 0, of which waited for: 2 -> 0; matrix products, arithmetic and copies ran while one was open for 2% -> 0% of each run, Pallas kernels for 0% -> 0%
where the time goes in v3:
time: 58.5 us; the launch traced here: 58.2 us
  Pallas kernels  53.1 us (91%)
  local copies, waits for them, and re-layouts  2.73 us (5%)
  between operations  2.39 us (4%)
    pallas_call x1, Pallas kernels, per_device(): pl.pallas_call(step_kernel, name='step', out_shape=(jax.ShapeDtypeStruct(...  53.1 us
    unnamed x2, local copies, waits for them, and re-layouts  2.73 us

profile of v3, /device:TPU:1, one launch (start us, length us, event | category | flops | bytes accessed | tf_op | source)
XLA Modules:
  0.0 58.2 jit_solution(17310487878966158167)
XLA Ops:
  0.6 53.1 %step.1 = (f32[24,128]{1,0:T(8,128)}, f32[3,3072]{1,0:T(4,128)}, f32[1,1]{1,0:T(1,128)}) custom-call(s32[14,24]{1,0:T(8,128)} %bitcast.5, s32[4,24]{1,0:T(4,128)} %bitcast.6, s32[7,6]{1,0:T(8,128)} %ghost_ref.1, s32[6]{0:T(128)} %count_ref.1, f32[8,3072]{1,0:T(8,128)} %own_ref.1, f32[4,768]{1,0:T(4,128)} %wall_ref.1), custom_call_target="tpu_custom_call" | custom-call | tf_op jit(solution)/shard_map/step/pallas_call | solution.py:412
  53.8 1.3 %copy.12 = f32[3072]{0:T(1024)} copy(f32[3072]{0:T(1024)} %bitcast.4) | data formatting | bytes 24576
  55.1 1.4 %copy.13 = f32[3,3072]{1,0:T(4,128)} copy(f32[3,3072]{1,0:T(4,128)} %get-tuple-element.13) | data formatting | bytes 73728

commit v4 on v3

--- a/solution.py
+++ b/solution.py
@@ -14,6 +14,8 @@
 NC = NB + 7 * GH
 NW = WB + 2 * EB
 LN = 128
+UNROLL = 4
+GROUP = 2
 
 smoothing = 0.1
 support = 0.3
@@ -91,14 +93,12 @@
     norm, flow = dot3(y, y), dot3(v, y)
     terms = split(stack(y + v + [half, zero]))
     sums = split(stack([norm, flow, one, one, one, zero, zero, zero]))
-    mixed = split(stack([half * c for c in y] + [half * norm, norm, one, one, one]))
-    base = [terms[j] for j, _ in CROSS]
     push = pressure_of(rho) / (rho * rho)
     heavy = stack(y + v + [flow, one]) * mass
     pushed = heavy * push
     hh, hl = two_terms(heavy)
     ph, pl_ = two_terms(pushed)
-    return wide(base + sums), wide(base + [mixed[j] for j, _ in CROSS]), stack([hh, ph, hl, pl_])
+    return wide([terms[j] for j, _ in CROSS] + sums), stack([hh, ph, hl, pl_])
 
 
 def wall_tiles(block):
@@ -114,29 +114,20 @@
 
 
 def target_tiles(block):
-    y, v, rho, mass = scaled_rows(block)
-    half = half_scale * rho
+    y, v, _, mass = scaled_rows(block)
     one, zero = jnp.ones_like(mass), jnp.zeros_like(mass)
     norm, flow = dot3(y, y), dot3(v, y)
-    reach = norm + eps_scaled
-    twice = [-2.0 * c for c in y]
-    far = split(stack(twice + [zero] * 5))
+    far = split(stack([-2.0 * c for c in y] + [zero] * 5))
     near = split(stack([-c for c in v] + [-c for c in y] + [zero] * 2))
-    damp = split(stack([half * c for c in twice] + [zero] * 3 + [reach, zero]))
-    mixed = split(stack(twice + [zero, half] + [zero] * 3))
-    norms, flows, grounds = split(norm), split(flow), split(half * reach)
-    mixed[0] = mixed[0] + stack([zero] * 3 + [one, zero] + grounds)
-    far_sum = stack([one, zero] + norms + [zero] * 3)
-    near_sum = stack([zero, one] + flows + [zero] * 3)
+    far_sum = stack([one, zero] + split(norm) + [zero] * 3)
+    near_sum = stack([zero, one] + split(flow) + [zero] * 3)
     return (
         wide([far[i] for _, i in CROSS] + [far_sum] * 3),
         wide([near[i] for _, i in CROSS] + [near_sum] * 3),
-        wide([damp[i] for _, i in CROSS] + [mixed[i] for _, i in CROSS]),
     )
 
 
 def falloff_of(dist_sq):
-    dist_sq = jnp.maximum(dist_sq, 1e-30)
     s = jnp.maximum(1.0 - dist_sq * lax.rsqrt(dist_sq), 0.0)
     return s, s * s * s
 
@@ -183,8 +174,8 @@
 def step_kernel(
     pair_ref, wpair_ref, ghost_ref, count_ref, own_ref, wall_ref, rate_ref, accel_ref, step_ref,
     blocks, outgoing, arrived, edges, edges_in, held, slots,
-    sf, se, sc, wf, wc, tf, te, tw, sums, wsums,
-    near0, near1, damp0, damp1, wall0, wall1, own_rows,
+    sf, sh, sc, wf, wc, tf, sums, wsums,
+    near0, near1, wall0, wall1, own_rows,
     send_sems, recv_sems, peak_send, peak_recv,
 ):
     orb = lax.axis_index("orb")
@@ -218,10 +209,14 @@
     lane = lax.broadcasted_iota(jnp.int32, (LN, 2 * LN), 1)
     doubled = jnp.where(row == lane // 32 * 16 + lane % 16, 1.0, 0.0).astype(BF16)
 
+    row = lax.broadcasted_iota(jnp.int32, (LN, LN), 0)
+    pick_half = jnp.where((row == 6) | (row == 30) | (row == 46), 1.0, 0.0).astype(BF16)
+
     def keep_source(j, block):
-        geometry, damping, columns = source_tiles(block)
-        sf[j] = geometry.astype(BF16).T
-        se[j] = damping.astype(BF16).T
+        geometry, columns = source_tiles(block)
+        tile = geometry.astype(BF16).T
+        sf[j] = tile
+        sh[j] = product(tile, pick_half)
         sc[j] = product(columns, doubled).astype(BF16)
 
     def build_own(b, carry):
@@ -234,15 +229,12 @@
         wc[b] = product(columns, doubled).astype(BF16)
 
     def build_target(b, carry):
-        distance, approach, damping = [t.astype(BF16) for t in target_tiles(blocks[b])]
-        zero = jnp.zeros((LN, LN), BF16)
-        tf[b] = jnp.concatenate([distance, approach], axis=1)
-        for ref, tile in ((te, damping), (tw, distance)):
-            ref[b, :LN, :LN] = tile
-            ref[b, :LN, LN:] = zero
-            ref[b, LN:, :LN] = zero
-            ref[b, LN:, LN:] = tile
+        tf[b] = jnp.concatenate([t.astype(BF16) for t in target_tiles(blocks[b])], axis=1)
         return carry
+
+    def diagonal(tile):
+        zero = jnp.zeros_like(tile)
+        return stack([jnp.concatenate([tile, zero], axis=1), jnp.concatenate([zero, tile], axis=1)])
 
     lax.fori_loop(0, NB, build_target, 0, unroll=2)
     for b in range(WB):
@@ -262,7 +254,7 @@
     for q in (6, 5, 3, 4, 2, 1, 0):
         ghost_copies[q].start()
 
-    lax.fori_loop(0, NB, build_own, 0, unroll=3)
+    lax.fori_loop(0, NB, build_own, 0, unroll=6)
     for copy in edge_copies:
         copy.wait()
     keep_wall(0, jnp.where(place > 0, edges_in[1], 0.0))
@@ -289,7 +281,7 @@
         for n in range(group):
             b = t * group + n
             tiles = paired(wf, [wpair_ref[k, b] for k in range(KW)])
-            wall[n * tall : (n + 1) * tall] = product(tiles, tw[b])
+            wall[n * tall : (n + 1) * tall] = product(tiles, diagonal(tf[b, :, :LN]))
 
     def wall_forces(t, wall):
         for n in range(group):
@@ -297,7 +289,7 @@
             total = jnp.zeros((16, 2 * LN), F32)
             for k in range(KW):
                 half, side = pl.ds(n * tall + k // 2 * LN, LN), k % 2 * LN
-                s, cubed = falloff_of(wall[half, side : side + LN])
+                s, cubed = falloff_of(jnp.maximum(wall[half, side : side + LN], 1e-30))
                 total += product(wc[wpair_ref[k, b]], matrix(cubed, cubed * s))
             wsums[b] = total[:8] + total[8:]
 
@@ -319,34 +311,36 @@
             keep_source(NB + q * GH + g, arrived[q, pl.ds(pl.multiple_of(g * 8, 8), 8), :])
             return carry
 
-        lax.fori_loop(0, GH, build_ghost, 0, unroll=3)
-
-    def geometry(b, near, damp):
-        indices = [pair_ref[k, b] for k in range(K)]
-        near[...] = product(gathered(sf, indices), tf[b])
-        damp[...] = product(paired(se, indices), te[b])
-
-    def forces(b, near, damp):
+        lax.fori_loop(0, GH, build_ghost, 0, unroll=6)
+
+    def geometry(b, near):
+        for n in range(0, K, GROUP):
+            indices = [pair_ref[k, b] for k in range(n, n + GROUP)]
+            near[pl.ds(n * LN, GROUP * LN), :] = product(gathered(sf, indices), tf[b])
+
+    def forces(b, near):
         total = jnp.zeros((32, 2 * LN), F32)
+        half = half_scale * blocks[b, 6:7, :]
         for k in range(K):
-            tile, half, side = pl.ds(k * LN, LN), pl.ds(k // 2 * LN, LN), k % 2 * LN
-            s, cubed = falloff_of(near[tile, :LN])
-            root = lax.rsqrt(damp[half, side : side + LN])
-            drag = jnp.minimum(near[tile, LN:], 0.0) * (root * root)
-            total += product(sc[pair_ref[k, b]], matrix(cubed, cubed * (drag - s)))
+            j, tile = pair_ref[k, b], pl.ds(k * LN, LN)
+            dist_sq = jnp.maximum(near[tile, :LN], 1e-30)
+            s, cubed = falloff_of(dist_sq)
+            damp = (dist_sq + eps_scaled) * (sh[j] + half)
+            drag = jnp.minimum(near[tile, LN:], 0.0) / damp
+            total += product(sc[j], matrix(cubed, cubed * (drag - s)))
         sums[b] = total[:16] + total[16:]
 
-    geometry(0, near0, damp0)
-
-    def two_blocks(t, carry):
-        b = 2 * t
-        geometry(b + 1, near1, damp1)
-        forces(b, near0, damp0)
-        geometry(jnp.minimum(b + 2, NB - 1), near0, damp0)
-        forces(b + 1, near1, damp1)
+    geometry(0, near0)
+    stages = near0, near1
+
+    def some_blocks(t, carry):
+        for n in range(UNROLL):
+            b = UNROLL * t + n
+            geometry(jnp.minimum(b + 1, NB - 1), stages[(n + 1) % 2])
+            forces(b, stages[n % 2])
         return carry
 
-    lax.fori_loop(0, NB // 2, two_blocks, 0)
+    lax.fori_loop(0, NB // UNROLL, some_blocks, 0)
 
     for b in range(NB):
         own_rows[8 * b : 8 * b + 8, :] = blocks[b]
@@ -428,18 +422,15 @@
             pltpu.VMEM((3, 1, LN), F32),
             pltpu.VMEM((2, 15, 1, LN), F32),
             pltpu.VMEM((NC, LN, LN), BF16),
-            pltpu.VMEM((NC, LN, LN), BF16),
+            pltpu.VMEM((NC, LN, LN), F32),
             pltpu.VMEM((NC, 32, 2 * LN), BF16),
             pltpu.VMEM((NW, LN, LN), BF16),
             pltpu.VMEM((NW, 16, 2 * LN), BF16),
             pltpu.VMEM((NB, LN, 2 * LN), BF16),
-            pltpu.VMEM((NB, 2 * LN, 2 * LN), BF16),
-            pltpu.VMEM((NB, 2 * LN, 2 * LN), BF16),
             pltpu.VMEM((NB, 16, 2 * LN), F32),
             pltpu.VMEM((NB, 8, 2 * LN), F32),
         ]
         + [pltpu.VMEM((K * LN, 2 * LN), F32)] * 2
-        + [pltpu.VMEM((K // 2 * LN, 2 * LN), F32)] * 2
         + [pltpu.VMEM((4 * KW // 2 * LN, 2 * LN), F32)] * 2
         + [
             pltpu.VMEM((NB * 8, LN), F32),

time: 58.5 us -> 56.8 us (0.971)
  Pallas kernels: 53.1 us -> 51.4 us
    pallas_call x1, Pallas kernels: 53.1 us -> 51.4 us  [per_device(): pl.pallas_call(step_kernel, name='step', out_shape=(jax.ShapeDtypeStruct(...]
where the time goes in v4:
time: 56.8 us; the launch traced here: 56.6 us
  Pallas kernels  51.4 us (90%)
  local copies, waits for them, and re-layouts  2.73 us (5%)
  between operations  2.39 us (4%)
    pallas_call x1, Pallas kernels, per_device(): pl.pallas_call(step_kernel, name='step', out_shape=(jax.ShapeDtypeStruct(...  51.4 us
    unnamed x2, local copies, waits for them, and re-layouts  2.73 us

profile of v4, /device:TPU:1, one launch (start us, length us, event | category | flops | bytes accessed | tf_op | source)
XLA Modules:
  0.0 56.6 jit_solution(16208514965641116851)
XLA Ops:
  0.6 51.4 %step.1 = (f32[24,128]{1,0:T(8,128)}, f32[3,3072]{1,0:T(4,128)}, f32[1,1]{1,0:T(1,128)}) custom-call(s32[14,24]{1,0:T(8,128)} %bitcast.5, s32[4,24]{1,0:T(4,128)} %bitcast.6, s32[7,6]{1,0:T(8,128)} %ghost_ref.1, s32[6]{0:T(128)} %count_ref.1, f32[8,3072]{1,0:T(8,128)} %own_ref.1, f32[4,768]{1,0:T(4,128)} %wall_ref.1), custom_call_target="tpu_custom_call" | custom-call | tf_op jit(solution)/shard_map/step/pallas_call | solution.py:406
  52.1 1.3 %copy.12 = f32[3072]{0:T(1024)} copy(f32[3072]{0:T(1024)} %bitcast.4) | data formatting | bytes 24576
  53.4 1.4 %copy.13 = f32[3,3072]{1,0:T(4,128)} copy(f32[3,3072]{1,0:T(4,128)} %get-tuple-element.13) | data formatting | bytes 73728

commit v5 on v4

--- a/solution.py
+++ b/solution.py
@@ -172,11 +172,12 @@
 
 
 def step_kernel(
-    pair_ref, wpair_ref, ghost_ref, count_ref, own_ref, wall_ref, rate_ref, accel_ref, step_ref,
+    pair_in, wpair_in, ghost_in, count_in, own_in, wall_in, rate_out, accel_out, step_ref,
+    pair_ref, wpair_ref, ghost_ref, count_ref, own_ref, wall_ref, rate_ref, accel_ref,
     blocks, outgoing, arrived, edges, edges_in, held, slots,
     sf, sh, sc, wf, wc, tf, sums, wsums,
     near0, near1, wall0, wall1, own_rows,
-    send_sems, recv_sems, peak_send, peak_recv,
+    send_sems, recv_sems, peak_send, peak_recv, load_sems, store_sems,
 ):
     orb = lax.axis_index("orb")
     place = lax.axis_index("wall")
@@ -186,11 +187,21 @@
     below = {"wall": lax.rem(place + places - 1, places)}
     phases = rounds()
 
+    sources = pair_in, wpair_in, ghost_in, count_in, own_in, wall_in
+    targets = pair_ref, wpair_ref, ghost_ref, count_ref, own_ref, wall_ref
+    loads = [
+        pltpu.make_async_copy(source, target, load_sems.at[n])
+        for n, (source, target) in enumerate(zip(sources, targets))
+    ]
+    for copy in loads:
+        copy.start()
     barrier = pltpu.get_barrier_semaphore()
     greeted = [*partners, above, below, *phases[0], *phases[1]]
     for device in greeted:
         pl.semaphore_signal(barrier, inc=1, device_id=device, device_id_type=MESH)
 
+    for copy in loads:
+        copy.wait()
     for b in range(NB):
         blocks[b] = own_ref[:, LN * b : LN * b + LN]
     for q in range(7):
@@ -209,18 +220,19 @@
     lane = lax.broadcasted_iota(jnp.int32, (LN, 2 * LN), 1)
     doubled = jnp.where(row == lane // 32 * 16 + lane % 16, 1.0, 0.0).astype(BF16)
 
-    row = lax.broadcasted_iota(jnp.int32, (LN, LN), 0)
-    pick_half = jnp.where((row == 6) | (row == 30) | (row == 46), 1.0, 0.0).astype(BF16)
-
-    def keep_source(j, block):
-        geometry, columns = source_tiles(block)
-        tile = geometry.astype(BF16).T
-        sf[j] = tile
-        sh[j] = product(tile, pick_half)
-        sc[j] = product(columns, doubled).astype(BF16)
-
-    def build_own(b, carry):
-        keep_source(b, blocks[b])
+    def keep_sources(first, group):
+        columns = []
+        for n, block in enumerate(group):
+            geometry, column = source_tiles(block)
+            sf[first + n] = geometry.astype(BF16).T
+            sh[first + n] = jnp.broadcast_to(half_scale * block[6:7], (LN, LN)).T
+            columns.append(column)
+        wide_columns = product(stack(columns), doubled).astype(BF16)
+        for n in range(len(group)):
+            sc[first + n] = wide_columns[32 * n : 32 * n + 32]
+
+    def build_own(t, carry):
+        keep_sources(t * GH, [blocks[t * GH + n] for n in range(GH)])
         return carry
 
     def keep_wall(b, block):
@@ -237,6 +249,7 @@
         return stack([jnp.concatenate([tile, zero], axis=1), jnp.concatenate([zero, tile], axis=1)])
 
     lax.fori_loop(0, NB, build_target, 0, unroll=2)
+    lax.fori_loop(0, NB // GH, build_own, 0)
     for b in range(WB):
         keep_wall(b + 1, live_block(b))
 
@@ -254,7 +267,6 @@
     for q in (6, 5, 3, 4, 2, 1, 0):
         ghost_copies[q].start()
 
-    lax.fori_loop(0, NB, build_own, 0, unroll=6)
     for copy in edge_copies:
         copy.wait()
     keep_wall(0, jnp.where(place > 0, edges_in[1], 0.0))
@@ -306,12 +318,7 @@
 
     for q in (0, 1, 2, 4, 3, 5, 6):
         ghost_copies[q].wait()
-
-        def build_ghost(g, carry, q=q):
-            keep_source(NB + q * GH + g, arrived[q, pl.ds(pl.multiple_of(g * 8, 8), 8), :])
-            return carry
-
-        lax.fori_loop(0, GH, build_ghost, 0, unroll=6)
+        keep_sources(NB + q * GH, [arrived[q, 8 * g : 8 * g + 8, :] for g in range(GH)])
 
     def geometry(b, near):
         for n in range(0, K, GROUP):
@@ -387,6 +394,12 @@
     for c in range(3):
         for b in range(NB):
             accel_ref[c : c + 1, LN * b : LN * b + LN] = forces_out[c][b : b + 1]
+    stores = [
+        pltpu.make_async_copy(rate_ref, rate_out, store_sems.at[0]),
+        pltpu.make_async_copy(accel_ref, accel_out, store_sems.at[1]),
+    ]
+    for copy in stores:
+        copy.start()
     for n in range(2):
         best = held[n]
         for t, copy in enumerate(copies):
@@ -398,10 +411,24 @@
             for copy in copies:
                 copy.start()
     step_ref[0, 0] = jnp.max(courant * jnp.sqrt(smoothing / (best + 1e-06)))
+    for copy in stores:
+        copy.wait()
+
+
+def handed_on(rates, acceleration):
+    def kernel(rate_ref, accel_ref, rate_out, accel_out):
+        rate_out[...] = rate_ref[...]
+        accel_out[...] = accel_ref[...]
+
+    vmem = pl.BlockSpec(memory_space=pltpu.VMEM)
+    shapes = jax.ShapeDtypeStruct((NB, LN), F32), jax.ShapeDtypeStruct((3, NB * LN), F32)
+    return pl.pallas_call(
+        kernel, name="handed_on", out_shape=shapes, in_specs=[vmem, vmem], out_specs=(vmem, vmem)
+    )(rates, acceleration)
 
 
 def per_device(fluid_state, ghost_list, pair_list, wall_state, wall_count, wall_pairs):
-    vmem = pl.BlockSpec(memory_space=pltpu.VMEM)
+    anywhere = pl.BlockSpec(memory_space=pl.ANY)
     smem = pl.BlockSpec(memory_space=pltpu.SMEM)
     rates, acceleration, step = pl.pallas_call(
         step_kernel,
@@ -411,9 +438,17 @@
             jax.ShapeDtypeStruct((3, NB * LN), F32),
             jax.ShapeDtypeStruct((1, 1), F32),
         ),
-        in_specs=[smem, smem, smem, smem, vmem, vmem],
-        out_specs=(vmem, vmem, smem),
+        in_specs=[anywhere] * 6,
+        out_specs=(anywhere, anywhere, smem),
         scratch_shapes=[
+            pltpu.SMEM((K, NB), jnp.int32),
+            pltpu.SMEM((KW, NB), jnp.int32),
+            pltpu.SMEM((7, GH), jnp.int32),
+            pltpu.SMEM((WB,), jnp.int32),
+            pltpu.VMEM((8, NB * LN), F32),
+            pltpu.VMEM((4, WB * LN), F32),
+            pltpu.VMEM((NB, LN), F32),
+            pltpu.VMEM((3, NB * LN), F32),
             pltpu.VMEM((NB, 8, LN), F32),
             pltpu.VMEM((7, GH * 8, LN), F32),
             pltpu.VMEM((7, GH * 8, LN), F32),
@@ -438,9 +473,12 @@
             pltpu.SemaphoreType.DMA((9,)),
             pltpu.SemaphoreType.DMA((2, 15)),
             pltpu.SemaphoreType.DMA((2, 15)),
+            pltpu.SemaphoreType.DMA((6,)),
+            pltpu.SemaphoreType.DMA((2,)),
         ],
         compiler_params=pltpu.CompilerParams(collective_id=0, has_side_effects=True),
     )(pair_list.T, wall_pairs.T, ghost_list, wall_count, fluid_state, wall_state)
+    rates, acceleration = handed_on(rates, acceleration)
     return (rates.reshape(-1), acceleration, step.reshape(()))
 
 

time: 56.8 us -> 53.8 us (0.947)
  local copies, waits for them, and re-layouts: 2.73 us -> 0 us
    unnamed x2 -> x0, local copies, waits for them, and re-layouts: 2.73 us -> none
    pallas_call x1, Pallas kernels: 51.4 us -> 49.7 us  [per_device(): pl.pallas_call(step_kernel, name='step', out_shape=(jax.ShapeDtypeStruct(...]
    pallas_call x0 -> x1, Pallas kernels: none -> 1.45 us  [handed_on(): pl.pallas_call(kernel, name='handed_on', out_shape=shapes, in_specs=[vmem...]
where the time goes in v5:
time: 53.8 us; the launch traced here: 53.5 us
  Pallas kernels  51.2 us (95%)
  between operations  2.33 us (4%)
    pallas_call x1, Pallas kernels, per_device(): pl.pallas_call(step_kernel, name='step', out_shape=(jax.ShapeDtypeStruct(...  49.7 us
    pallas_call x1, Pallas kernels, handed_on(): pl.pallas_call(kernel, name='handed_on', out_shape=shapes, in_specs=[vmem...  1.45 us

profile of v5, /device:TPU:1, one launch (start us, length us, event | category | flops | bytes accessed | tf_op | source)
XLA Modules:
  0.0 53.5 jit_solution(18316211857072173374)
XLA Ops:
  0.6 49.7 %step.1 = (f32[24,128]{1,0:T(8,128)}, f32[3,3072]{1,0:T(4,128)}, f32[1,1]{1,0:T(1,128)}) custom-call(s32[14,24]{1,0:T(8,128)} %bitcast.4, s32[4,24]{1,0:T(4,128)} %bitcast.5, s32[7,6]{1,0:T(8,128)} %ghost_in.1, s32[6]{0:T(128)} %count_in.1, f32[8,3072]{1,0:T(8,128)} %own_in.1, f32[4,768]{1,0:T(4,128)} %wall_in.1), custom_call_target="tpu_custom_call" | custom-call | tf_op jit(solution)/shard_map/step/pallas_call | solution.py:433
  50.4 1.4 %handed_on.1 = (f32[24,128]{1,0:T(8,128)}, f32[3,3072]{1,0:T(4,128)}) custom-call(f32[24,128]{1,0:T(8,128)} %get-tuple-element.8.rate_ref, f32[3,3072]{1,0:T(4,128)} %get-tuple-element.9.accel_ref), custom_call_target="tpu_custom_call" | custom-call | tf_op jit(solution)/shard_map/handed_on/pallas_call | solution.py:425

commit v6 on v5

--- a/solution.py
+++ b/solution.py
@@ -15,6 +15,7 @@
 NW = WB + 2 * EB
 LN = 128
 UNROLL = 4
+WALL_LAG = 12
 GROUP = 2
 
 smoothing = 0.1
@@ -196,7 +197,8 @@
     for copy in loads:
         copy.start()
     barrier = pltpu.get_barrier_semaphore()
-    greeted = [*partners, above, below, *phases[0], *phases[1]]
+    far_first = sorted(range(15), key=lambda t: abs(t - 7))
+    greeted = [phases[n][t] for t in far_first for n in range(2)] + [*partners, above, below]
     for device in greeted:
         pl.semaphore_signal(barrier, inc=1, device_id=device, device_id_type=MESH)
 
@@ -295,23 +297,29 @@
             tiles = paired(wf, [wpair_ref[k, b] for k in range(KW)])
             wall[n * tall : (n + 1) * tall] = product(tiles, diagonal(tf[b, :, :LN]))
 
-    def wall_forces(t, wall):
+    def wall_forces(t, wall, at):
+        past = []
         for n in range(group):
             b = t * group + n
             total = jnp.zeros((16, 2 * LN), F32)
             for k in range(KW):
+                if len(past) >= WALL_LAG:
+                    row = pl.multiple_of(group * tall + 16 * at, 16)
+                    wall[pl.ds(row, 16), :] = past[len(past) - WALL_LAG]
                 half, side = pl.ds(n * tall + k // 2 * LN, LN), k % 2 * LN
                 s, cubed = falloff_of(jnp.maximum(wall[half, side : side + LN], 1e-30))
                 total += product(wc[wpair_ref[k, b]], matrix(cubed, cubed * s))
+                past.append(total)
             wsums[b] = total[:8] + total[8:]
 
     wall_geometry(0, wall0)
 
     def two_walls(t, carry):
         wall_geometry(2 * t + 1, wall1)
-        wall_forces(2 * t, wall0)
+        at = lax.div(t, NB)
+        wall_forces(2 * t, wall0, at)
         wall_geometry(jnp.minimum(2 * t + 2, NB // group - 1), wall0)
-        wall_forces(2 * t + 1, wall1)
+        wall_forces(2 * t + 1, wall1, at)
         return carry
 
     lax.fori_loop(0, NB // group // 2, two_walls, 0)
@@ -466,7 +474,7 @@
             pltpu.VMEM((NB, 8, 2 * LN), F32),
         ]
         + [pltpu.VMEM((K * LN, 2 * LN), F32)] * 2
-        + [pltpu.VMEM((4 * KW // 2 * LN, 2 * LN), F32)] * 2
+        + [pltpu.VMEM((4 * KW // 2 * LN + 32, 2 * LN), F32)] * 2
         + [
             pltpu.VMEM((NB * 8, LN), F32),
             pltpu.SemaphoreType.DMA((9,)),

time: 53.8 us -> 52.9 us (0.983)
  Pallas kernels: 51.2 us -> 50.3 us
    pallas_call x1, Pallas kernels: 49.7 us -> 48.9 us  [per_device(): pl.pallas_call(step_kernel, name='step', out_shape=(jax.ShapeDtypeStruct(...]
where the time goes in v6:
time: 52.9 us; the launch traced here: 52.6 us
  Pallas kernels  50.3 us (95%)
  between operations  2.33 us (4%)
    pallas_call x1, Pallas kernels, per_device(): pl.pallas_call(step_kernel, name='step', out_shape=(jax.ShapeDtypeStruct(...  48.9 us
    pallas_call x1, Pallas kernels, handed_on(): pl.pallas_call(kernel, name='handed_on', out_shape=shapes, in_specs=[vmem...  1.45 us

profile of v6, /device:TPU:1, one launch (start us, length us, event | category | flops | bytes accessed | tf_op | source)
XLA Modules:
  0.0 52.6 jit_solution(1485416656318146647)
XLA Ops:
  0.6 48.9 %step.1 = (f32[24,128]{1,0:T(8,128)}, f32[3,3072]{1,0:T(4,128)}, f32[1,1]{1,0:T(1,128)}) custom-call(s32[14,24]{1,0:T(8,128)} %bitcast.4, s32[4,24]{1,0:T(4,128)} %bitcast.5, s32[7,6]{1,0:T(8,128)} %ghost_in.1, s32[6]{0:T(128)} %count_in.1, f32[8,3072]{1,0:T(8,128)} %own_in.1, f32[4,768]{1,0:T(4,128)} %wall_in.1), custom_call_target="tpu_custom_call" | custom-call | tf_op jit(solution)/shard_map/step/pallas_call | solution.py:441
  49.5 1.4 %handed_on.1 = (f32[24,128]{1,0:T(8,128)}, f32[3,3072]{1,0:T(4,128)}) custom-call(f32[24,128]{1,0:T(8,128)} %get-tuple-element.8.rate_ref, f32[3,3072]{1,0:T(4,128)} %get-tuple-element.9.accel_ref), custom_call_target="tpu_custom_call" | custom-call | tf_op jit(solution)/shard_map/handed_on/pallas_call | solution.py:433

commit v7 on v6

--- a/solution.py
+++ b/solution.py
@@ -148,16 +148,24 @@
     return partner
 
 
+def farthest_first(long, short):
+    steps = [(i, j) for i in range(long) for j in range(short) if i or j]
+    return sorted(steps, key=lambda step: -min(step[0], long - step[0]) - min(step[1], short - step[1]))
+
+
 def rounds():
     orb = lax.axis_index("orb")
     place = lax.axis_index("wall")
     x, rest = lax.div(orb, 16), lax.rem(orb, 16)
-    mine = x * 4 + place
-    first = []
-    for t in range(1, 16):
-        other = lax.rem(mine + t, 16)
-        first.append({"orb": lax.div(other, 4) * 16 + rest, "wall": lax.rem(other, 4)})
-    second = [{"orb": x * 16 + lax.rem(rest + t, 16), "wall": place} for t in range(1, 16)]
+    z, core = lax.div(rest, 2), lax.rem(rest, 2)
+    first = [
+        {"orb": lax.rem(x + i, 4) * 16 + rest, "wall": lax.rem(place + j, 4)}
+        for i, j in farthest_first(4, 4)
+    ]
+    second = [
+        {"orb": x * 16 + lax.rem(z + i, 8) * 2 + lax.rem(core + j, 2), "wall": place}
+        for i, j in farthest_first(8, 2)
+    ]
     return first, second
 
 
@@ -197,8 +205,7 @@
     for copy in loads:
         copy.start()
     barrier = pltpu.get_barrier_semaphore()
-    far_first = sorted(range(15), key=lambda t: abs(t - 7))
-    greeted = [phases[n][t] for t in far_first for n in range(2)] + [*partners, above, below]
+    greeted = [device for pair in zip(*phases) for device in pair] + [*partners, above, below]
     for device in greeted:
         pl.semaphore_signal(barrier, inc=1, device_id=device, device_id_type=MESH)
 
@@ -410,7 +417,7 @@
         copy.start()
     for n in range(2):
         best = held[n]
-        for t, copy in enumerate(copies):
+        for t, copy in reversed(list(enumerate(copies))):
             copy.wait()
             best = jnp.maximum(best, slots[n, t])
         held[n + 1] = best

time: 52.9 us -> 52.7 us (level)
  no operation moved by 1% of the time
where the time goes in v7:
time: 52.7 us; the launch traced here: 52.5 us
  Pallas kernels  50.1 us (95%)
  between operations  2.33 us (4%)
    pallas_call x1, Pallas kernels, per_device(): pl.pallas_call(step_kernel, name='step', out_shape=(jax.ShapeDtypeStruct(...  48.7 us
    pallas_call x1, Pallas kernels, handed_on(): pl.pallas_call(kernel, name='handed_on', out_shape=shapes, in_specs=[vmem...  1.45 us

profile of v7, /device:TPU:1, one launch (start us, length us, event | category | flops | bytes accessed | tf_op | source)
XLA Modules:
  0.0 52.5 jit_solution(5997183769252038474)
XLA Ops:
  0.6 48.7 %step.1 = (f32[24,128]{1,0:T(8,128)}, f32[3,3072]{1,0:T(4,128)}, f32[1,1]{1,0:T(1,128)}) custom-call(s32[14,24]{1,0:T(8,128)} %bitcast.4, s32[4,24]{1,0:T(4,128)} %bitcast.5, s32[7,6]{1,0:T(8,128)} %ghost_in.1, s32[6]{0:T(128)} %count_in.1, f32[8,3072]{1,0:T(8,128)} %own_in.1, f32[4,768]{1,0:T(4,128)} %wall_in.1), custom_call_target="tpu_custom_call" | custom-call | tf_op jit(solution)/shard_map/step/pallas_call | solution.py:448
  49.3 1.4 %handed_on.1 = (f32[24,128]{1,0:T(8,128)}, f32[3,3072]{1,0:T(4,128)}) custom-call(f32[24,128]{1,0:T(8,128)} %get-tuple-element.8.rate_ref, f32[3,3072]{1,0:T(4,128)} %get-tuple-element.9.accel_ref), custom_call_target="tpu_custom_call" | custom-call | tf_op jit(solution)/shard_map/handed_on/pallas_call | solution.py:440

commit v8 on v7

--- a/solution.py
+++ b/solution.py
@@ -257,7 +257,7 @@
         zero = jnp.zeros_like(tile)
         return stack([jnp.concatenate([tile, zero], axis=1), jnp.concatenate([zero, tile], axis=1)])
 
-    lax.fori_loop(0, NB, build_target, 0, unroll=2)
+    lax.fori_loop(0, NB, build_target, 0, unroll=6)
     lax.fori_loop(0, NB // GH, build_own, 0)
     for b in range(WB):
         keep_wall(b + 1, live_block(b))

time: 52.7 us -> 52.7 us (level)
  no operation moved by 1% of the time
where the time goes in v8:
time: 52.7 us; the launch traced here: 52.5 us
  Pallas kernels  50.1 us (95%)
  between operations  2.33 us (4%)
    pallas_call x1, Pallas kernels, per_device(): pl.pallas_call(step_kernel, name='step', out_shape=(jax.ShapeDtypeStruct(...  48.7 us
    pallas_call x1, Pallas kernels, handed_on(): pl.pallas_call(kernel, name='handed_on', out_shape=shapes, in_specs=[vmem...  1.45 us

profile of v8, /device:TPU:1, one launch (start us, length us, event | category | flops | bytes accessed | tf_op | source)
XLA Modules:
  0.0 52.5 jit_solution(4563303693267437560)
XLA Ops:
  0.6 48.7 %step.1 = (f32[24,128]{1,0:T(8,128)}, f32[3,3072]{1,0:T(4,128)}, f32[1,1]{1,0:T(1,128)}) custom-call(s32[14,24]{1,0:T(8,128)} %bitcast.4, s32[4,24]{1,0:T(4,128)} %bitcast.5, s32[7,6]{1,0:T(8,128)} %ghost_in.1, s32[6]{0:T(128)} %count_in.1, f32[8,3072]{1,0:T(8,128)} %own_in.1, f32[4,768]{1,0:T(4,128)} %wall_in.1), custom_call_target="tpu_custom_call" | custom-call | tf_op jit(solution)/shard_map/step/pallas_call | solution.py:448
  49.3 1.4 %handed_on.1 = (f32[24,128]{1,0:T(8,128)}, f32[3,3072]{1,0:T(4,128)}) custom-call(f32[24,128]{1,0:T(8,128)} %get-tuple-element.8.rate_ref, f32[3,3072]{1,0:T(4,128)} %get-tuple-element.9.accel_ref), custom_call_target="tpu_custom_call" | custom-call | tf_op jit(solution)/shard_map/handed_on/pallas_call | solution.py:440
